TPU v7x, 32 devices: a whole 2x2x4 slice. The times are simulated.
32 devices in a mesh: dp: 8 (over z, x), tensor: 4 (over y, core).
Axes of the slice: x: 2, y: 2, z: 4, core: 2. Of those that a mesh axis runs over, the one named last changes fastest.
Arguments:
- tokens: bfloat16 [4096, 1024], P(('dp', 'tensor')), may hold values from -6 to 6
- cotangent: bfloat16 [4096, 1024], P(('dp', 'tensor')), may hold values from -6 to 6
- norm1_gain: bfloat16 [1024], P('dp'), may hold values from 0.5 to 1.5
- w_query: bfloat16 [1024, 1024], P('dp', 'tensor'), may hold values from -0.1875 to 0.1875
- w_key: bfloat16 [1024, 1024], P('dp', 'tensor'), may hold values from -0.1875 to 0.1875
- w_value: bfloat16 [1024, 2048], P('dp', 'tensor'), may hold values from -0.1875 to 0.1875
- w_gate_out: bfloat16 [1024, 2048], P('dp', 'tensor'), may hold values from -0.1875 to 0.1875
- w_out: bfloat16 [1024, 2048], P('dp', 'tensor'), may hold values from -0.1875 to 0.1875
- w_beta: bfloat16 [1024, 8], P('dp', 'tensor'), may hold values from -0.1875 to 0.1875
- w_alpha: bfloat16 [1024, 8], P('dp', 'tensor'), may hold values from -0.1875 to 0.1875
- conv_query: bfloat16 [128, 8, 4], P('dp', 'tensor'), may hold values from -3 to 3
- conv_key: bfloat16 [128, 8, 4], P('dp', 'tensor'), may hold values from -3 to 3
- conv_value: bfloat16 [256, 8, 4], P('dp', 'tensor'), may hold values from -3 to 3
- a_log: bfloat16 [8], P('tensor'), may hold values from 0 to 2.765625
- dt_bias: bfloat16 [8], P('tensor'), may hold values from -6.875 to -2.296875
- head_gain: bfloat16 [256, 8], P('dp', 'tensor'), may hold values from 0.5 to 1.5
- norm2_gain: bfloat16 [1024], P('dp'), may hold values from 0.5 to 1.5
- w_up_gate: bfloat16 [1024, 2816], P('dp', 'tensor'), may hold values from -0.1875 to 0.1875
- w_up: bfloat16 [1024, 2816], P('dp', 'tensor'), may hold values from -0.1875 to 0.1875
- w_down: bfloat16 [1024, 2816], P('dp', 'tensor'), may hold values from -0.109375 to 0.109375
Outputs:
- out: bfloat16 [4096, 1024], P(('dp', 'tensor'))
- grad_tokens: float32 [4096, 1024], P(('dp', 'tensor'))
- grad_norm1_gain: float32 [1024], P('dp')
- grad_w_query: float32 [1024, 1024], P('dp', 'tensor')
- grad_w_key: float32 [1024, 1024], P('dp', 'tensor')
- grad_w_value: float32 [1024, 2048], P('dp', 'tensor')
- grad_w_gate_out: float32 [1024, 2048], P('dp', 'tensor')
- grad_w_out: float32 [1024, 2048], P('dp', 'tensor')
- grad_w_beta: float32 [1024, 8], P('dp', 'tensor')
- grad_w_alpha: float32 [1024, 8], P('dp', 'tensor')
- grad_conv_query: float32 [128, 8, 4], P('dp', 'tensor')
- grad_conv_key: float32 [128, 8, 4], P('dp', 'tensor')
- grad_conv_value: float32 [256, 8, 4], P('dp', 'tensor')
- grad_a_log: float32 [8], P('tensor')
- grad_dt_bias: float32 [8], P('tensor')
- grad_head_gain: float32 [256, 8], P('dp', 'tensor')
- grad_norm2_gain: float32 [1024], P('dp')
- grad_w_up_gate: float32 [1024, 2816], P('dp', 'tensor')
- grad_w_up: float32 [1024, 2816], P('dp', 'tensor')
- grad_w_down: float32 [1024, 2816], P('dp', 'tensor')
All inputs are finite; a program needn't handle non-finite values.
Results may differ from a plain program's by a relative error of at most 0.012.
Values may be sent and summed in bfloat16 or wider, within the bound.
A program may use at most 128 MiB of HBM per device.

v0:
```python
import jax
import jax.numpy as jnp
from jax import lax
from jax.experimental import pallas as pl
from jax.experimental.pallas import tpu as pltpu
from jax.sharding import PartitionSpec as P

epsilon = 1e-06
CHUNK = 128
LANES = 128
contract_rows = (((0,), (0,)), ((), ()))
contract_cols = (((1,), (1,)), ((), ()))
contract_plain = (((1,), (0,)), ((), ()))
highest = lax.Precision.HIGHEST


def norm_forward(row_values):
    row_scale = lax.rsqrt(jnp.mean(row_values * row_values, axis=-1, keepdims=True) + epsilon)
    return (row_scale, row_values * row_scale)


def norm_backward(grad_normed, unit_values, row_scale, gain_values):
    grad_unit = grad_normed * gain_values
    return row_scale * (
        grad_unit - unit_values * jnp.mean(grad_unit * unit_values, axis=-1, keepdims=True)
    )


def weight_grad(left_in, right_in):
    return lax.dot_general(left_in, right_in, contract_rows, preferred_element_type=jnp.float32)


def times_transpose(left_in, right_in):
    return lax.dot_general(left_in, right_in, contract_cols, preferred_element_type=jnp.float32)


def fine_dot(left_in, right_in, dims=contract_plain):
    return lax.dot_general(
        left_in, right_in, dims, precision=lax.Precision.HIGH, preferred_element_type=jnp.float32
    )


def exact_dot(left_in, right_in, dims=contract_plain):
    return fine_dot(left_in, right_in, dims)


def silu(values):
    return values * lax.logistic(values)


def unit_length(values):
    return values * lax.rsqrt(jnp.sum(values * values, axis=-1, keepdims=True) + epsilon)


def triangle_masks(size):
    row = lax.broadcasted_iota(jnp.int32, (size, size), 0)
    col = lax.broadcasted_iota(jnp.int32, (size, size), 1)
    return row, col


def unit_lower_inverses(lowers):
    size = lowers[0].shape[0]
    row, col = triangle_masks(size)
    eye = jnp.where(row == col, 1.0, 0.0)
    inverses = [eye for _ in lowers]
    bit = 0
    while (1 << bit) < size:
        joined = ((row >> (bit + 1)) == (col >> (bit + 1))) & ((row >> bit) != (col >> bit))
        parts = [jnp.where(joined, lower, 0.0) for lower in lowers]
        if bit == 0:
            inverses = [eye - part for part in parts]
        else:
            inner = [fine_dot(part, inverse) for part, inverse in zip(parts, inverses)]
            steps = [fine_dot(inverse, step) for inverse, step in zip(inverses, inner)]
            inverses = [inverse - step for inverse, step in zip(inverses, steps)]
        bit += 1
    return inverses


@jax.custom_vjp
def known_inverse(lower, inverse):
    return inverse


def known_inverse_fwd(lower, inverse):
    return inverse, inverse


def known_inverse_bwd(inverse, grad):
    turned = inverse.T
    return -fine_dot(fine_dot(turned, grad), turned), jnp.zeros_like(inverse)


known_inverse.defvjp(known_inverse_fwd, known_inverse_bwd)


def each(call, *lists):
    return [call(*items) for items in zip(*lists)]


def mixer_chunk(conv_q, conv_k, conv_v, proj_gate, beta, gate, gain, state, inverter):
    size, key_dim = conv_q[0].shape
    row, col = triangle_masks(size)
    strict = row > col
    lower = row >= col
    query = each(lambda v: unit_length(silu(v)) * key_dim ** (-0.5), conv_q)
    key = each(lambda v: unit_length(silu(v)), conv_k)
    value = each(silu, conv_v)
    wide = each(lambda g: jnp.broadcast_to(g, (size, size)), gate)
    decay_col = each(
        lambda w: jnp.sum(jnp.where(lower, w.T, 0.0), axis=1, keepdims=True), wide
    )
    decay_row = each(
        lambda w: jnp.sum(jnp.where(row <= col, w, 0.0), axis=0, keepdims=True), wide
    )
    decay_end = each(lambda g: jnp.sum(g, axis=0, keepdims=True), gate)
    differ = each(lambda c, r: jnp.where(strict, c - r, 0.0), decay_col, decay_row)
    decay = each(lambda d: jnp.where(lower, jnp.exp(d), 0.0), differ)
    grams = each(lambda k: exact_dot(k, k, contract_cols), key)
    system = each(lambda g, d, b: jnp.where(strict, g * d * b, 0.0), grams, decay, beta)
    inverse = inverter(system)
    grown = each(jnp.exp, decay_col)
    kept = each(lambda k, b, g, s: exact_dot(k * (b * g), s), key, beta, grown, state)
    fresh = each(lambda i, v, b, k: exact_dot(i, v * b - k), inverse, value, beta, kept)
    scores = each(lambda q, k, d: exact_dot(q, k, contract_cols) * d, query, key, decay)
    carried = each(lambda q, g, s: exact_dot(q * g, s), query, grown, state)
    mixed = each(lambda c, s, f: c + exact_dot(s, f), carried, scores, fresh)
    added = each(
        lambda k, e, c, f: exact_dot(k * jnp.exp(e - c), f, contract_rows),
        key, decay_end, decay_col, fresh,
    )
    new_state = each(lambda e, s, a: jnp.exp(e) * s + a, decay_end, state, added)
    gated = each(
        lambda m, g, p: m
        * lax.rsqrt(jnp.mean(m * m, axis=-1, keepdims=True) + epsilon)
        * g
        * silu(p),
        mixed, gain, proj_gate,
    )
    return gated, new_state, inverse


def head_slices(head, heads, key_dim, value_dim):
    q_at = head * key_dim
    k_at = (heads + head) * key_dim
    v_at = 2 * heads * key_dim + head * value_dim
    return (
        slice(q_at, q_at + key_dim),
        slice(k_at, k_at + key_dim),
        slice(v_at, v_at + value_dim),
        slice(head * value_dim, (head + 1) * value_dim),
    )


def head_inputs(heads, key_dim, value_dim, conv_ref, pgate_ref, rates_ref, gain_ref):
    at = [head_slices(head, heads, key_dim, value_dim) for head in range(heads)]
    return at, (
        [conv_ref[:, spots[0]] for spots in at],
        [conv_ref[:, spots[1]] for spots in at],
        [conv_ref[:, spots[2]] for spots in at],
        [pgate_ref[:, spots[3]] for spots in at],
        [rates_ref[:, head : head + 1] for head in range(heads)],
        [rates_ref[:, heads + head : heads + head + 1] for head in range(heads)],
        [gain_ref[:, spots[3]] for spots in at],
    )


def mixer_forward_kernel(
    heads, key_dim, value_dim, conv_ref, pgate_ref, rates_ref, gain_ref,
    gated_ref, states_ref, inverses_ref, state_ref,
):
    @pl.when(pl.program_id(0) == 0)
    def _():
        state_ref[...] = jnp.zeros_like(state_ref)

    at, operands = head_inputs(
        heads, key_dim, value_dim, conv_ref, pgate_ref, rates_ref, gain_ref
    )
    state = [state_ref[head] for head in range(heads)]
    gated, new_state, inverse = mixer_chunk(*operands, state, unit_lower_inverses)
    for head in range(heads):
        gated_ref[:, at[head][3]] = gated[head].astype(gated_ref.dtype)
        states_ref[0, head] = state[head]
        inverses_ref[0, head] = inverse[head]
        state_ref[head] = new_state[head]


def mixer_backward_kernel(
    heads, key_dim, value_dim, conv_ref, pgate_ref, rates_ref, gain_ref, states_ref,
    inverses_ref, grad_ref, gconv_ref, gpgate_ref, grates_ref, ggain_ref, gstate_ref,
):
    @pl.when(pl.program_id(0) == 0)
    def _():
        gstate_ref[...] = jnp.zeros_like(gstate_ref)
        ggain_ref[...] = jnp.zeros_like(ggain_ref)

    lane = lax.broadcasted_iota(jnp.int32, grates_ref.shape, 1)
    rates_grad = jnp.zeros(grates_ref.shape, jnp.float32)
    at, operands = head_inputs(
        heads, key_dim, value_dim, conv_ref, pgate_ref, rates_ref, gain_ref
    )
    inverses = [inverses_ref[0, head] for head in range(heads)]

    def run(*operands):
        gated, new_state, _ = mixer_chunk(
            *operands, lambda systems: each(known_inverse, systems, inverses)
        )
        return gated, new_state

    _, pull = jax.vjp(run, *operands, [states_ref[0, head] for head in range(heads)])
    pulled = pull(
        (
            [grad_ref[:, spots[3]] for spots in at],
            [gstate_ref[head] for head in range(heads)],
        )
    )
    for head in range(heads):
        at_q, at_k, at_v, at_g = at[head]
        gconv_ref[:, at_q] = pulled[0][head]
        gconv_ref[:, at_k] = pulled[1][head]
        gconv_ref[:, at_v] = pulled[2][head]
        gpgate_ref[:, at_g] = pulled[3][head]
        rates_grad = jnp.where(lane == head, pulled[4][head], rates_grad)
        rates_grad = jnp.where(lane == heads + head, pulled[5][head], rates_grad)
        ggain_ref[:, at_g] += pulled[6][head]
        gstate_ref[head] = pulled[7][head]
    grates_ref[...] = rates_grad


def row_block(width, order):
    return pl.BlockSpec((CHUNK, width), lambda step: (order(step), 0))


def mixer_forward(conv_all, proj_gate, rates, gain_row, heads, key_dim, value_dim):
    rows, conv_width = conv_all.shape
    steps = rows // CHUNK
    forward = lambda step: step
    width = heads * value_dim
    return pl.pallas_call(
        lambda *refs: mixer_forward_kernel(heads, key_dim, value_dim, *refs),
        name="mixer_forward",
        grid=(steps,),
        in_specs=[
            row_block(conv_width, forward),
            row_block(width, forward),
            row_block(rates.shape[1], forward),
            pl.BlockSpec((1, width), lambda step: (0, 0)),
        ],
        out_specs=[
            row_block(width, forward),
            pl.BlockSpec((1, heads, key_dim, value_dim), lambda step: (step, 0, 0, 0)),
            pl.BlockSpec((1, heads, CHUNK, CHUNK), lambda step: (step, 0, 0, 0)),
        ],
        out_shape=[
            jax.ShapeDtypeStruct((rows, width), jnp.bfloat16),
            jax.ShapeDtypeStruct((steps, heads, key_dim, value_dim), jnp.float32),
            jax.ShapeDtypeStruct((steps, heads, CHUNK, CHUNK), jnp.float32),
        ],
        scratch_shapes=[pltpu.VMEM((heads, key_dim, value_dim), jnp.float32)],
        cost_estimate=pl.CostEstimate(
            flops=30_000_000_000, bytes_accessed=8_000_000, transcendentals=1_000_000
        ),
    )(conv_all, proj_gate, rates, gain_row)


def mixer_backward(
    conv_all, proj_gate, rates, gain_row, states, inverses, grad_gated, heads, key_dim, value_dim
):
    rows, conv_width = conv_all.shape
    steps = rows // CHUNK
    back = lambda step: steps - 1 - step
    width = heads * value_dim
    return pl.pallas_call(
        lambda *refs: mixer_backward_kernel(heads, key_dim, value_dim, *refs),
        name="mixer_backward",
        grid=(steps,),
        in_specs=[
            row_block(conv_width, back),
            row_block(width, back),
            row_block(rates.shape[1], back),
            pl.BlockSpec((1, width), lambda step: (0, 0)),
            pl.BlockSpec((1, heads, key_dim, value_dim), lambda step: (back(step), 0, 0, 0)),
            pl.BlockSpec((1, heads, CHUNK, CHUNK), lambda step: (back(step), 0, 0, 0)),
            row_block(width, back),
        ],
        out_specs=[
            row_block(conv_width, back),
            row_block(width, back),
            row_block(rates.shape[1], back),
            pl.BlockSpec((1, width), lambda step: (0, 0)),
        ],
        out_shape=[
            jax.ShapeDtypeStruct((rows, conv_width), jnp.float32),
            jax.ShapeDtypeStruct((rows, width), jnp.float32),
            jax.ShapeDtypeStruct(rates.shape, jnp.float32),
            jax.ShapeDtypeStruct((1, width), jnp.float32),
        ],
        scratch_shapes=[pltpu.VMEM((heads, key_dim, value_dim), jnp.float32)],
        cost_estimate=pl.CostEstimate(
            flops=30_000_000_000, bytes_accessed=12_000_000, transcendentals=2_000_000
        ),
    )(conv_all, proj_gate, rates, gain_row, states, inverses, grad_gated)


def ring_position(index, size):
    if size % 2:
        return index
    side, line = index % 2, index // 2
    return line + side * (size - 1 - 2 * line)


def ring_index(position, size):
    if size % 2:
        return position
    side = position // (size // 2)
    line = position + side * (size - 1 - 2 * position)
    return line * 2 + side


def greet(peers):
    barrier = pltpu.get_barrier_semaphore()
    for target in peers:
        pl.semaphore_signal(
            barrier, inc=1, device_id=target, device_id_type=pl.DeviceIdType.MESH
        )
    pl.semaphore_wait(barrier, len(peers))


def send(source, place, sent, landed, target):
    copy = pltpu.make_async_remote_copy(
        src_ref=source,
        dst_ref=place,
        send_sem=sent,
        recv_sem=landed,
        device_id=target,
        device_id_type=pl.DeviceIdType.MESH,
    )
    copy.start()
    return copy


def others(axis):
    ranks = lax.axis_size(axis)
    mine = lax.axis_index(axis)
    return [lax.rem(mine + step, ranks) for step in range(1, ranks)]


def ring_ends(dp):
    at = ring_position(lax.axis_index("dp"), dp)
    after = ring_index((at + 1) % dp, dp)
    before = ring_index((at + dp - 1) % dp, dp)
    return at, after, before


def gather_kernel(dp, ranks, widths, count, *refs):
    parts = len(widths) + 1
    shards, rows = refs[:parts], refs[parts : parts + count]
    full_ref, small_ref = refs[parts + count : parts + count + 2]
    gots = refs[parts + count + 2 : parts + 2 * count + 2]
    own_sems, ring_sent, ring_got, row_sent, row_got = refs[parts + 2 * count + 2 :]
    me, mine = lax.axis_index("dp"), lax.axis_index("tensor")
    at, after, before = ring_ends(dp)
    peers = others("tensor")
    ends = [{"dp": after}, {"dp": before}]
    greet(ends + [{"tensor": peer} for peer in peers])
    lefts = [sum(widths[:part]) for part in range(parts)]
    hops = [[(dp - 1 + (part + way) % 2) // 2 for part in range(parts)] for way in range(2)]

    def place(owner, part):
        if part == parts - 1:
            return small_ref.at[owner]
        return full_ref.at[owner, :, pl.ds(lefts[part], widths[part])]

    flying = {}

    def hop(way, step, part):
        owner = ring_index((at + (dp - step if way == 0 else step)) % dp, dp)
        spot = place(owner, part)
        flying[way, step, part] = send(
            shards[part] if step == 0 else spot,
            spot,
            ring_sent.at[way, step, part],
            ring_got.at[way, step, part],
            ends[way],
        )

    for part in range(parts):
        for way in range(2):
            if hops[way][part] > 0:
                hop(way, 0, part)
    swaps = []
    for step, peer in enumerate(peers):
        for index in range(count):
            swaps.append(
                send(
                    rows[index],
                    gots[index].at[mine],
                    row_sent.at[step, index],
                    row_got.at[step, index],
                    {"tensor": peer},
                )
            )
    local = []
    for part in range(parts):
        local.append(pltpu.make_async_copy(shards[part], place(me, part), own_sems.at[part]))
    for index in range(count):
        local.append(
            pltpu.make_async_copy(rows[index], gots[index].at[mine], own_sems.at[parts + index])
        )
    for copy in local:
        copy.start()
    for step in range(1, max(max(line) for line in hops) + 1):
        for part in range(parts):
            for way in range(2):
                if hops[way][part] >= step:
                    flying[way, step - 1, part].wait_recv()
                    if hops[way][part] > step:
                        hop(way, step, part)
    for copy in local + swaps:
        copy.wait()
    for copy in flying.values():
        copy.wait_send()


def gather_all(shards, small, rows, number):
    dp, ranks = lax.axis_size("dp"), lax.axis_size("tensor")
    widths = [shard.shape[1] for shard in shards]
    parts, count = len(shards) + 1, len(rows)
    anywhere = pl.BlockSpec(memory_space=pl.ANY)
    vmem = pl.BlockSpec(memory_space=pltpu.VMEM)
    sem = pltpu.SemaphoreType.DMA
    got = pl.pallas_call(
        lambda *refs: gather_kernel(dp, ranks, widths, count, *refs),
        name="gather_all",
        in_specs=[anywhere] * (parts + count),
        out_specs=[vmem] * (2 + count),
        out_shape=[
            jax.ShapeDtypeStruct((dp, shards[0].shape[0], sum(widths)), shards[0].dtype),
            jax.ShapeDtypeStruct((dp,) + small.shape, small.dtype),
        ]
        + [jax.ShapeDtypeStruct((ranks,) + block.shape, block.dtype) for block in rows],
        scratch_shapes=[
            sem((parts + count,)),
            sem((2, max(1, dp // 2), parts)),
            sem((2, max(1, dp // 2), parts)),
            sem((ranks - 1, count)),
            sem((ranks - 1, count)),
        ],
        compiler_params=pltpu.CompilerParams(collective_id=number, has_side_effects=True),
        cost_estimate=pl.CostEstimate(
            flops=30_000_000_000, bytes_accessed=16_000_000, transcendentals=0
        ),
    )(*shards, small, *rows)
    full = got[0].reshape(-1, sum(widths))
    return full, got[1], [block.reshape(-1, block.shape[-1]) for block in got[2:]]


def reduce_kernel(dp, ranks, lines, count, *refs):
    arrays = count[0]
    grads, swaps_in, tile_ref = refs[:arrays], refs[arrays : arrays + count[1]], refs[arrays + count[1]]
    refs = refs[arrays + count[1] + 1 :]
    sums, swaps_out = refs[:arrays], refs[arrays : arrays + count[1]]
    tiles_ref, lines_ref = refs[arrays + count[1] : arrays + count[1] + 2]
    refs = refs[arrays + count[1] + 2 :]
    landed, totals = refs[:arrays], refs[arrays : 2 * arrays]
    ring_sent, ring_got, row_sent, row_got, tile_sent, tile_got, line_sent, line_got = refs[
        2 * arrays :
    ]
    me, mine = lax.axis_index("dp"), lax.axis_index("tensor")
    at, after, before = ring_ends(dp)
    peers, mates = others("tensor"), others("dp")
    ends = [{"dp": after}, {"dp": before}]
    greet([{"dp": mate} for mate in mates] + [{"tensor": peer} for peer in peers])
    last = dp - 2

    def owner(way, step):
        return ring_index((at + (2 * dp - 1 - step if way == 0 else 1 + step)) % dp, dp)

    flying = {}

    def hop(line, step):
        array, top, rows, way = lines[line]
        span = pl.ds(top, rows)
        source = grads[array].at[owner(way, 0), span] if step == 0 else totals[array].at[step - 1, span]
        flying[line, step] = send(
            source,
            landed[array].at[step, span],
            ring_sent.at[line, step],
            ring_got.at[line, step],
            ends[way],
        )

    for line in range(len(lines)):
        hop(line, 0)
    copies = []
    for step, mate in enumerate(mates):
        copies.append(
            send(tile_ref, tiles_ref.at[me], tile_sent.at[step], tile_got.at[step], {"dp": mate})
        )
    for index in range(count[1]):
        for step, peer in enumerate(peers):
            copies.append(
                send(
                    swaps_in[index].at[peer],
                    swaps_out[index].at[mine],
                    row_sent.at[step, index],
                    row_got.at[step, index],
                    {"tensor": peer},
                )
            )
    tiles_ref[me] = tile_ref[...]
    for index in range(count[1]):
        swaps_out[index][mine] = swaps_in[index][mine]
    for step in range(dp - 1):
        for line, (array, top, rows, way) in enumerate(lines):
            flying[line, step].wait_recv()
            span = pl.ds(top, rows)
            own = me if step == last else owner(way, step + 1)
            total = landed[array][step, span].astype(jnp.float32) + grads[array][
                own, span
            ].astype(jnp.float32)
            if step == last:
                sums[array][span] = total
            else:
                totals[array][step, span] = total.astype(totals[array].dtype)
                hop(line, step + 1)
    small = sums[arrays - 1]
    for step, peer in enumerate(peers):
        copies.append(
            send(small, lines_ref.at[mine], line_sent.at[step], line_got.at[step], {"tensor": peer})
        )
    lines_ref[mine] = small[...]
    for copy in copies:
        copy.wait()
    for copy in flying.values():
        copy.wait_send()


def reduce_all(grads, swaps, tile, number):
    dp, ranks = lax.axis_size("dp"), lax.axis_size("tensor")
    vmem = pl.BlockSpec(memory_space=pltpu.VMEM)
    sem = pltpu.SemaphoreType.DMA
    lines = []
    for array, grad in enumerate(grads):
        rows = grad.shape[1]
        pieces = 4 if rows * grad.shape[2] > 100_000 and rows % 64 == 0 else 2
        for piece in range(pieces):
            lines.append((array, piece * rows // pieces, rows // pieces, piece % 2))
    lines = lines[-2:] + lines[:-2]
    count = (len(grads), len(swaps))
    inputs = list(grads) + list(swaps) + [tile]
    small = grads[-1].shape[1:]
    results = pl.pallas_call(
        lambda *refs: reduce_kernel(dp, ranks, lines, count, *refs),
        name="reduce_all",
        in_specs=[vmem] * len(inputs),
        out_specs=[vmem] * (len(inputs) + 1),
        out_shape=[jax.ShapeDtypeStruct(grad.shape[1:], jnp.float32) for grad in grads]
        + [jax.ShapeDtypeStruct(block.shape, block.dtype) for block in swaps]
        + [
            jax.ShapeDtypeStruct((dp,) + tile.shape, tile.dtype),
            jax.ShapeDtypeStruct((ranks,) + small, jnp.float32),
        ],
        scratch_shapes=[pltpu.VMEM((dp - 1,) + grad.shape[1:], grad.dtype) for grad in grads]
        + [pltpu.VMEM((dp - 1,) + grad.shape[1:], grad.dtype) for grad in grads]
        + [
            sem((len(lines), dp - 1)),
            sem((len(lines), dp - 1)),
            sem((ranks - 1, len(swaps))),
            sem((ranks - 1, len(swaps))),
            sem((dp - 1,)),
            sem((dp - 1,)),
            sem((ranks - 1,)),
            sem((ranks - 1,)),
        ],
        compiler_params=pltpu.CompilerParams(collective_id=number, has_side_effects=True),
        cost_estimate=pl.CostEstimate(
            flops=30_000_000_000, bytes_accessed=16_000_000, transcendentals=0
        ),
    )(*inputs)
    arrays = len(grads)
    return results[:arrays], results[arrays : arrays + len(swaps)], results[-2], results[-1]


def forward_finish(summed, tokens_ref, gain_ref, middle_ref, span):
    middle = tokens_ref[span].astype(jnp.float32) + summed
    middle_ref[span] = middle
    _, unit = norm_forward(middle)
    return unit * gain_ref[...]


def backward_finish(summed, cotangent_ref, gain_ref, middle_ref, grad_ref, gain_grad_ref, span):
    scale, unit = norm_forward(middle_ref[span])
    gain_grad_ref[...] += jnp.sum(summed * unit, axis=0, keepdims=True)
    grad = cotangent_ref[span].astype(jnp.float32) + norm_backward(
        summed, unit, scale, gain_ref[...]
    )
    grad_ref[span] = grad
    return grad


def turn_kernel(ranks, chunks, backward, *refs):
    if backward:
        part_ref, rows_ref, gain_ref, middle_ref, got_ref, grad_ref, gain_grad_ref = refs[:7]
        scratch = refs[7:]
        gain_grad_ref[...] = jnp.zeros_like(gain_grad_ref)
    else:
        part_ref, rows_ref, gain_ref, got_ref, middle_ref = refs[:5]
        scratch = refs[5:]
    pair_buf, sum_buf, far_buf, pair_s, pair_r, far_s, far_r, out_s, out_r, on_s, on_r = scratch
    mine = lax.axis_index("tensor")
    side, group = mine % 2, mine // 2
    groups = ranks // 2
    partner = group * 2 + 1 - side
    away = [(group + step) % groups for step in range(1, groups)]
    mates = [{"tensor": other * 2 + side} for other in away]
    near = {"tensor": partner}
    greet([near] + mates)
    rows = part_ref.shape[1] // chunks
    flying = []
    spans = [pl.ds(chunk * rows, rows) for chunk in range(chunks)]

    def go(*operands):
        copy = send(*operands)
        flying.append(copy)
        return copy

    pairs, fars, outs, ons, backs = {}, {}, {}, {}, {}
    order = away + [group]
    for chunk, span in enumerate(spans):
        for step, other in enumerate(order):
            pairs[step, chunk] = go(
                part_ref.at[other * 2 + 1 - side, span],
                pair_buf.at[step, span],
                pair_s.at[step, chunk],
                pair_r.at[step, chunk],
                near,
            )
    for chunk, span in enumerate(spans):
        for step, other in enumerate(away):
            pairs[step, chunk].wait_recv()
            total = part_ref[other * 2 + side, span].astype(jnp.float32) + pair_buf[
                step, span
            ].astype(jnp.float32)
            sum_buf[step, span] = total.astype(sum_buf.dtype)
            fars[step, chunk] = go(
                sum_buf.at[step, span],
                far_buf.at[step, span],
                far_s.at[step, chunk],
                far_r.at[step, chunk],
                mates[step],
            )
    for chunk, span in enumerate(spans):
        pairs[groups - 1, chunk].wait_recv()
        summed = part_ref[mine, span].astype(jnp.float32) + pair_buf[groups - 1, span].astype(
            jnp.float32
        )
        for step in range(groups - 1):
            fars[step, chunk].wait_recv()
            summed = summed + far_buf[step, span].astype(jnp.float32)
        if backward:
            done = backward_finish(
                summed, rows_ref, gain_ref, middle_ref, grad_ref, gain_grad_ref, span
            )
        else:
            done = forward_finish(summed, rows_ref, gain_ref, middle_ref, span)
        got_ref[mine, span] = done.astype(got_ref.dtype)
        place = got_ref.at[mine, span]
        for step in range(groups - 1):
            outs[step, chunk] = go(
                place, place, out_s.at[step, chunk], out_r.at[step, chunk], mates[step]
            )
        ons[groups - 1, chunk] = go(
            place, place, on_s.at[groups - 1, chunk], on_r.at[groups - 1, chunk], near
        )
    for chunk, span in enumerate(spans):
        for step in range(groups - 1):
            outs[step, chunk].wait_recv()
            source = ((group + groups - 1 - step) % groups) * 2 + side
            place = got_ref.at[source, span]
            ons[step, chunk] = go(
                place, place, on_s.at[step, chunk], on_r.at[step, chunk], near
            )
    for chunk in range(chunks):
        for step in range(groups):
            ons[step, chunk].wait_recv()
    for copy in flying:
        copy.wait_send()


def turn(part, own_rows, gain, number, middle=None, chunks=4):
    ranks = lax.axis_size("tensor")
    rows, model = own_rows.shape
    chunks = chunks if rows % (16 * chunks) == 0 else 1
    groups = ranks // 2
    backward = middle is not None
    vmem = pl.BlockSpec(memory_space=pltpu.VMEM)
    sem = pltpu.SemaphoreType.DMA
    out_shape = [
        jax.ShapeDtypeStruct((ranks, rows, model), jnp.bfloat16),
        jax.ShapeDtypeStruct((rows, model), jnp.float32),
    ]
    inputs = [part.reshape(ranks, rows, model), own_rows, gain]
    if backward:
        out_shape.append(jax.ShapeDtypeStruct((1, model), jnp.float32))
        inputs.append(middle)
    results = pl.pallas_call(
        lambda *refs: turn_kernel(ranks, chunks, backward, *refs),
        name="turn_backward" if backward else "turn_forward",
        in_specs=[vmem] * len(inputs),
        out_specs=[vmem] * len(out_shape),
        out_shape=out_shape,
        scratch_shapes=[
            pltpu.VMEM((groups, rows, model), jnp.bfloat16),
            pltpu.VMEM((max(1, groups - 1), rows, model), jnp.bfloat16),
            pltpu.VMEM((max(1, groups - 1), rows, model), jnp.bfloat16),
        ]
        + [sem((groups, chunks))] * 8,
        compiler_params=pltpu.CompilerParams(collective_id=number, has_side_effects=True),
        cost_estimate=pl.CostEstimate(
            flops=10_000_000_000, bytes_accessed=4_000_000, transcendentals=0
        ),
    )(*inputs)
    return (results[0].reshape(-1, model),) + tuple(results[1:])


def short_conv(inputs, weights):
    tap_count = weights.shape[0]
    row_count = inputs.shape[0]
    padded = jnp.pad(inputs, ((tap_count - 1, 0), (0, 0)))
    result = jnp.zeros_like(inputs)
    for offset in range(tap_count):
        result = result + padded[offset : offset + row_count] * weights[offset]
    return result


def round_up(size, step):
    return -(-size // step) * step


def pad_columns(matrix_in, width):
    return jnp.pad(matrix_in, ((0, 0), (0, width - matrix_in.shape[1])))


def tap_rows(conv_weights):
    channels, heads, taps = conv_weights.shape
    return jnp.transpose(conv_weights, (1, 2, 0)).reshape(heads * taps, channels)


def joined_taps(rows, heads):
    shards, _, channels = rows.shape
    split = rows.reshape(shards, heads, -1, channels)
    taps = split.shape[2]
    return jnp.transpose(split, (2, 1, 0, 3)).reshape(taps, heads * shards * channels)


def split_taps(taps_in, heads, shards):
    taps, width = taps_in.shape
    split = taps_in.reshape(taps, heads, shards, width // (heads * shards))
    return jnp.transpose(split, (2, 1, 0, 3)).reshape(shards, heads * taps, -1)


def rate_terms(proj_beta, proj_alpha, log_rate, rate_bias):
    log_gates = -jnp.exp(log_rate) * jax.nn.softplus(proj_alpha + rate_bias)
    return jnp.concatenate([jax.nn.sigmoid(proj_beta), log_gates], axis=1)


def on_device(
    tokens, cotangent, norm1_gain, w_query, w_key, w_value, w_gate_out, w_out, w_beta, w_alpha,
    conv_query, conv_key, conv_value, a_log, dt_bias, head_gain, norm2_gain, w_up_gate, w_up,
    w_down,
):
    bf16, f32 = jnp.bfloat16, jnp.float32
    shard_rows, model = w_query.shape[0], tokens.shape[1]
    dp = model // shard_rows
    heads = a_log.shape[0]
    key_dim, value_dim = w_query.shape[1] // heads, w_value.shape[1] // heads
    taps = conv_query.shape[2]
    tap_lines = heads * taps
    qk_width, v_width = heads * key_dim, heads * value_dim
    conv_width = 2 * qk_width + v_width
    in_width = conv_width + v_width
    hidden_width = w_up.shape[1]
    ff = round_up(hidden_width, 256)

    packed = [tap_rows(conv_query), tap_rows(conv_key), tap_rows(conv_value), head_gain.T]
    lanes = [block.shape[1] for block in packed]
    lefts = [sum(lanes[:index]) for index in range(4)]
    line_rows = tap_lines + 2 + 2 * heads
    small_rows = round_up(line_rows, 16)
    small_width = round_up(max(sum(lanes), shard_rows), LANES)

    def small_block(groups, lines, kind):
        shards = groups[0].shape[0]
        group = jnp.concatenate(
            [jnp.pad(g, ((0, 0), (0, tap_lines - g.shape[1]), (0, 0))) for g in groups], axis=2
        )
        group = jnp.pad(group, ((0, 0), (0, 0), (0, small_width - sum(lanes))))
        lines = jnp.pad(lines, ((0, 0), (0, 0), (0, small_width - lines.shape[2])))
        rest = jnp.zeros((shards, small_rows - line_rows, small_width), kind)
        return jnp.concatenate([group.astype(kind), lines.astype(kind), rest], axis=1)

    small = small_block(
        [block[None] for block in packed],
        jnp.concatenate([norm1_gain[None], norm2_gain[None], w_beta.T, w_alpha.T], axis=0)[None],
        bf16,
    )[0]
    ffn_pack = jnp.concatenate([pad_columns(w, ff) for w in (w_up_gate, w_up, w_down)], axis=1)
    out_full = lax.all_gather(w_out, "dp", axis=0, tiled=True)
    out_full, ffn_pack = lax.optimization_barrier((out_full, ffn_pack))
    ffn_full = lax.all_gather(ffn_pack, "dp", axis=0, tiled=True)
    in_full, small_full, (tokens_got, cot_full) = gather_all(
        [w_query, w_key, w_value, w_gate_out], small, [tokens, cotangent], 1
    )
    small_all = small_full.astype(f32)

    def group_of(index, rows):
        return small_all[:, :rows, lefts[index] : lefts[index] + lanes[index]]

    def line_of(first, count):
        lines = small_all[:, tap_lines + first : tap_lines + first + count, :shard_rows]
        return jnp.swapaxes(lines, 0, 1).reshape(count, model)

    gain_one, gain_two = line_of(0, 1), line_of(1, 1)
    rate_weights = line_of(2, 2 * heads).astype(bf16)
    conv_weights = jnp.concatenate(
        [joined_taps(group_of(index, tap_lines), heads) for index in range(3)], axis=1
    )
    gain_row = joined_taps(group_of(3, heads), heads)

    tokens_full = tokens_got.astype(f32)
    _, unit_full = norm_forward(tokens_full)
    normed_one = (unit_full * gain_one).astype(bf16)
    projected = jnp.dot(normed_one, in_full, preferred_element_type=f32)
    proj_rates = times_transpose(normed_one, rate_weights)
    proj_conv = projected[:, :conv_width]
    proj_gate = projected[:, conv_width:]
    conv_all, conv_pull = jax.vjp(short_conv, proj_conv, conv_weights)
    rates, rates_pull = jax.vjp(
        rate_terms, proj_rates[:, :heads], proj_rates[:, heads:], a_log.astype(f32),
        dt_bias.astype(f32),
    )
    mixed, states, inverses = mixer_forward(
        conv_all, proj_gate, rates, gain_row, heads, key_dim, value_dim
    )
    row_values = tokens.astype(f32)
    scale_one, unit_one = norm_forward(row_values)
    normed_two, middle = turn(
        times_transpose(mixed, out_full).astype(bf16), tokens, gain_two, 2
    )
    gates_full, down_full = ffn_full[:, : 2 * ff], ffn_full[:, 2 * ff :]
    grad_hidden = jnp.dot(cot_full, down_full, preferred_element_type=f32)
    ups = jnp.dot(normed_two, gates_full, preferred_element_type=f32)
    up_gate, up_lin = ups[:, :ff], ups[:, ff:]
    gate_sigmoid = jax.nn.sigmoid(up_gate)
    hidden = (up_gate * gate_sigmoid * up_lin).astype(bf16)
    grad_gate = (
        grad_hidden * up_lin * gate_sigmoid * (1.0 + up_gate * (1.0 - gate_sigmoid))
    ).astype(bf16)
    grad_lin = (grad_hidden * up_gate * gate_sigmoid).astype(bf16)
    grad_ups = jnp.concatenate([grad_gate, grad_lin], axis=1)
    ffn_grads = jnp.concatenate(
        [
            weight_grad(normed_two, grad_ups).astype(bf16),
            weight_grad(cot_full, hidden).astype(bf16),
        ],
        axis=1,
    )
    grad_normed_part_two = times_transpose(grad_ups, gates_full).astype(bf16)
    grad_normed_part_two, ffn_grads = lax.optimization_barrier((grad_normed_part_two, ffn_grads))
    ffn_sums = lax.psum_scatter(ffn_grads, "dp", scatter_dimension=0, tiled=True)
    mid_full, grad_middle, grad_gain_two = turn(
        grad_normed_part_two, cotangent, gain_two, 3, middle
    )
    ranks = lax.axis_size("tensor")
    out_grads = weight_grad(mid_full, mixed).astype(bf16)
    result_part = times_transpose(hidden, down_full).astype(bf16)

    grad_mixed = jnp.dot(mid_full, out_full, preferred_element_type=f32)
    grad_conv_all, grad_pgate, grad_rates, grad_gain_row = mixer_backward(
        conv_all, proj_gate, rates, gain_row, states, inverses, grad_mixed,
        heads, key_dim, value_dim,
    )
    grad_pconv, grad_conv_w = conv_pull(grad_conv_all)
    grad_beta, grad_alpha, grad_rate_part, grad_bias_part = rates_pull(grad_rates)
    grad_proj = jnp.concatenate([grad_pconv.astype(bf16), grad_pgate.astype(bf16)], axis=1)
    grad_rate_proj = jnp.concatenate([grad_beta, grad_alpha], axis=1).astype(bf16)
    grad_normed_part = times_transpose(grad_proj, in_full) + jnp.dot(
        grad_rate_proj, rate_weights, preferred_element_type=f32
    )
    grad_gain_one = jnp.sum(grad_normed_part * unit_full, axis=0)
    grad_lines = jnp.concatenate(
        [grad_gain_one[None], grad_gain_two, weight_grad(grad_rate_proj, normed_one)], axis=0
    )
    edges = [0, qk_width, 2 * qk_width, conv_width]
    grad_small = small_block(
        [split_taps(grad_conv_w[:, edges[i] : edges[i + 1]], heads, dp) for i in range(3)]
        + [split_taps(grad_gain_row, heads, dp)],
        jnp.swapaxes(grad_lines.reshape(2 + 2 * heads, dp, shard_rows), 0, 1),
        f32,
    )
    rate_line = jnp.concatenate([grad_rate_part, grad_bias_part])
    rate_tile = jnp.pad(rate_line[None], ((0, 7), (0, LANES - 2 * heads)))
    in_grads = weight_grad(normed_one, grad_proj).astype(bf16)
    sums, swapped, rate_tiles, small_lines = reduce_all(
        [
            in_grads.reshape(dp, shard_rows, in_width),
            out_grads.reshape(dp, shard_rows, v_width),
            grad_small,
        ],
        [
            grad_normed_part.astype(bf16).reshape(ranks, -1, model),
            result_part.reshape(ranks, -1, model),
        ],
        rate_tile,
        7,
    )
    in_sums, out_sums, small_sums = sums
    grad_normed_one = jnp.sum(swapped[0].astype(f32), axis=0)
    result = (middle + jnp.sum(swapped[1].astype(f32), axis=0)).astype(bf16)
    grad_rows = grad_middle + norm_backward(grad_normed_one, unit_one, scale_one, gain_one)
    rate_sums = jnp.sum(rate_tiles, axis=0)[0]
    gain_sums = jnp.sum(small_lines[:, tap_lines : tap_lines + 2, :shard_rows], axis=0)
    ffn_sums = ffn_sums.astype(f32)

    def taps_out(index, lines):
        block = small_sums[:lines, lefts[index] : lefts[index] + lanes[index]]
        return jnp.transpose(block.reshape(heads, -1, lanes[index]), (2, 0, 1))

    def lines_out(first):
        return small_sums[tap_lines + first : tap_lines + first + heads, :shard_rows].T

    return (
        result,
        grad_rows,
        gain_sums[0],
        in_sums[:, :qk_width],
        in_sums[:, qk_width : 2 * qk_width],
        in_sums[:, 2 * qk_width : conv_width],
        in_sums[:, conv_width:],
        out_sums,
        lines_out(2),
        lines_out(2 + heads),
        taps_out(0, tap_lines),
        taps_out(1, tap_lines),
        taps_out(2, tap_lines),
        rate_sums[:heads],
        rate_sums[heads : 2 * heads],
        taps_out(3, heads)[:, :, 0],
        gain_sums[1],
        ffn_sums[:, :hidden_width],
        ffn_sums[:, ff : ff + hidden_width],
        ffn_sums[:, 2 * ff : 2 * ff + hidden_width],
    )


def solution(mesh):
    placed = (
        P(("dp", "tensor"), None),
        P(("dp", "tensor"), None),
        P("dp"),
        P("dp", "tensor"),
        P("dp", "tensor"),
        P("dp", "tensor"),
        P("dp", "tensor"),
        P("dp", "tensor"),
        P("dp", "tensor"),
        P("dp", "tensor"),
        P("dp", "tensor", None),
        P("dp", "tensor", None),
        P("dp", "tensor", None),
        P("tensor"),
        P("tensor"),
        P("dp", "tensor"),
        P("dp"),
        P("dp", "tensor"),
        P("dp", "tensor"),
        P("dp", "tensor"),
    )
    return jax.shard_map(
        on_device,
        mesh=mesh,
        in_specs=placed,
        out_specs=(
            P(("dp", "tensor"), None),
            P(("dp", "tensor"), None),
            P("dp"),
            P("dp", "tensor"),
            P("dp", "tensor"),
            P("dp", "tensor"),
            P("dp", "tensor"),
            P("dp", "tensor"),
            P("dp", "tensor"),
            P("dp", "tensor"),
            P("dp", "tensor", None),
            P("dp", "tensor", None),
            P("dp", "tensor", None),
            P("tensor"),
            P("tensor"),
            P("dp", "tensor"),
            P("dp"),
            P("dp", "tensor"),
            P("dp", "tensor"),
            P("dp", "tensor"),
        ),
        check_vma=False,
    )
```

profile of v0, /device:TPU:0, one launch (start us, length us, event | category | flops | bytes accessed | tf_op | source)
XLA Modules:
  0.0 347.4 jit_solution(15593029081768997228)
XLA Ops:
  10.3 2.0 fusion.19
  12.2 40.9 %all-gather.3.cloned.1.call-done = bf16[1024,512]{1,0:T(8,128)(2,1)} async-done(((bf16[128,512]{1,0:T(8,128)(2,1)}), bf16[1024,512]{1,0:T(8,128)(2,1)}) %all-gather.3.cloned.1.call-update) | async-done | bytes 1048592 | tf_op jit(solution)/shard_map/all_gather | solution.py:809
  53.2 55.2 %gather_all.1 = (bf16[8,128,1536]{2,1,0:T(8,128)(2,1)}, bf16[8,16,128]{2,1,0:T(8,128)(2,1)}, bf16[4,128,1024]{2,1,0:T(8,128)(2,1)}, bf16[4,128,1024]{2,1,0:T(8,128)(2,1)}) custom-call(bf16[128,256]{1,0:T(8,128)(2,1)} %refs_0_.1, bf16[128,256]{1,0:T(8,128)(2,1)} %refs_1_.3, bf16[128,512]{1,0:T(8,128)(2,1)} %refs_2_.1, bf16[128,512]{1,0:T(8,128)(2,1)} %refs_3_.1, ...), custom_call_target="tpu_custom_call" | custom-call | flops 30000001024 | bytes 16000000 | tf_op jit(solution)/shard_map/gather_all/pallas_call | solution.py:432
  111.1 1.5 multiply_reduce_fusion.5
  113.2 1.5 multiply_convert_fusion.1
  114.8 1.8 fusion.61
  116.6 1.1 slice.195.refs_1_
  125.5 2.2 multiply_add_fusion.refs_0_
  127.7 17.2 %mixer_forward.1 = (bf16[512,512]{1,0:T(8,128)(2,1)}, f32[4,2,128,256]{3,2,1,0:T(8,128)}, f32[4,2,128,128]{3,2,1,0:T(8,128)}) custom-call(f32[512,1024]{1,0:T(8,128)} %multiply_add_fusion.refs_0_, f32[512,512]{1,0:T(8,128)} %slice.195.refs_1_, f32[512,4]{1,0:T(8,128)} %pad_maximum_fusion.7.refs_2_, f32[1,512]{1,0:T(1,128)} %reshape.232.refs_3_), custom_call_target="tpu_custom_call" | custom-call | flops 30000001024 | bytes 8000000 | tf_op jit(solution)/shard_map/mixer_forward/pallas_call | solution.py:239
  144.9 2.8 convolution_convert_fusion.5
  147.7 18.5 %turn_forward.1 = (bf16[4,128,1024]{2,1,0:T(8,128)(2,1)}, f32[128,1024]{1,0:T(8,128)}) custom-call(bf16[4,128,1024]{2,1,0:T(8,128)(2,1)} %bitcast.212, bf16[128,1024]{1,0:T(8,128)(2,1)} %refs_1_.4, f32[1,1024]{1,0:T(1,128)} %slice_bitcast_fusion.1.refs_2_), custom_call_target="tpu_custom_call" | custom-call | flops 10000000000 | bytes 4000000 | tf_op jit(solution)/shard_map/turn_forward/pallas_call | solution.py:707
  166.3 4.1 %fusion.2 = f32[512,1536]{1,0:T(8,128)S(1)} fusion(bf16[512,1024]{1,0:T(8,128)(2,1)} %bitcast.209, bf16[1024,2304]{0,1:T(8,128)(2,1)} %all-gather.5.cloned.1.call-done), kind=kOutput, calls=%fused_computation.5 | convolution fusion | flops 1610612736 | bytes 7340032 | tf_op jit(solution)/shard_map/dot_general | solution.py:853
  170.4 3.0 multiply_convert_fusion.4
  175.4 1.8 convolution_convert_fusion.1
  177.3 2.5 pad_maximum_fusion
  179.8 5.2 %fusion.5 = bf16[512,1024]{1,0:T(8,128)(2,1)} fusion(bf16[1024,2304]{0,1:T(8,128)(2,1)} %all-gather.5.cloned.1.call-done, bf16[512,768]{1,0:T(8,128)(2,1)} %copy-done.33, bf16[512,768]{1,0:T(8,128)(2,1)} %copy-done.32), kind=kOutput, calls=%fused_computation.36 | convolution fusion | flops 1614282752 | bytes 5767168 | tf_op jit(solution)/shard_map/dot_general | solution.py:34
  185.0 19.6 %turn_backward.1 = (bf16[4,128,1024]{2,1,0:T(8,128)(2,1)}, f32[128,1024]{1,0:T(8,128)}, f32[1,1024]{1,0:T(1,128)}) custom-call(bf16[4,128,1024]{2,1,0:T(8,128)(2,1)} %bitcast.211, bf16[128,1024]{1,0:T(8,128)(2,1)} %refs_1_.5, f32[1,1024]{1,0:T(1,128)} %slice_bitcast_fusion.1.refs_2_, f32[128,1024]{1,0:T(8,128)} %get-tuple-element.52.refs_3_), custom_call_target="tpu_custom_call" | custom-call | flops 10000000000 | bytes 4000000 | tf_op jit(solution)/shard_map/turn_backward/pallas_call | solution.py:707
  204.5 3.0 fusion.62.refs_6_
  207.5 18.1 %mixer_backward.1 = (f32[512,1024]{1,0:T(8,128)}, f32[512,512]{1,0:T(8,128)}, f32[512,4]{1,0:T(8,128)}, f32[1,512]{1,0:T(1,128)}) custom-call(f32[512,1024]{1,0:T(8,128)} %multiply_add_fusion.refs_0_, f32[512,512]{1,0:T(8,128)} %slice.195.refs_1_, f32[512,4]{1,0:T(8,128)} %pad_maximum_fusion.7.refs_2_, f32[1,512]{1,0:T(1,128)} %reshape.232.refs_3_, ...), custom_call_target="tpu_custom_call" | custom-call | flops 30000001024 | bytes 12000000 | tf_op jit(solution)/shard_map/mixer_backward/pallas_call | solution.py:273
  225.6 2.7 fusion.52
  229.5 1.3 reduce.4
  234.3 5.4 %multiply_reduce_fusion.3 = (f32[1024]{0:T(1024)S(1)}, f32[1024]{0:T(1024)S(1)}, f32[1024]{0:T(1024)S(1)}, f32[1024]{0:T(1024)S(1)}, f32[512,1024]{1,0:T(8,128)}...) fusion(f32[512,1024]{1,0:T(8,128)} %get-tuple-element.60, f32[512,1024]{1,0:T(8,128)S(1)} %slice.187, ...), kind=kLoop, calls=%fused_computation.17 | loop fusion | flops 6287360 | bytes 14712832 | tf_op jit(solution)/shard_map/transpose(jvp())/reduce_sum | solution.py:733
  240.0 4.8 %fusion.4 = bf16[512,1024]{1,0:T(8,128)(2,1)S(1)} fusion(f32[512,1024]{1,0:T(8,128)} %get-tuple-element.185, f32[512,1024]{1,0:T(8,128)} %get-tuple-element.186, f32[512,1024]{1,0:T(8,128)} %get-tuple-element.187, f32[512,1024]{1,0:T(8,128)} %get-tuple-element.188), kind=kLoop, calls=%fused_computation.8 | loop fusion | flops 2097152 | bytes 9437184 | tf_op jit(solution)/shard_map/convert.3
  245.0 1.9 fusion.15
  246.8 1.8 fusion.54
  250.7 3.1 convolution_convert_fusion.4
  253.7 3.5 convolution_convert_fusion.3
  257.2 3.5 %convolution_convert_fusion = bf16[1024,1536]{1,0:T(8,128)(2,1)} fusion(bf16[512,1024]{1,0:T(8,128)(2,1)S(1)} %get-tuple-element.189, bf16[512,512]{1,0:T(8,128)(2,1)S(1)} %copy-done.8, bf16[512,1024]{1,0:T(8,128)(2,1)S(1)} %fusion.4), kind=kOutput, calls=%fused_computation.1 | convolution fusion | flops 1615331328 | bytes 5767168 | tf_op jit(solution)/shard_map/dot_general | solution.py:30
  260.7 63.9 %reduce_all.1 = (f32[128,1536]{1,0:T(8,128)}, f32[128,512]{1,0:T(8,128)}, f32[16,128]{1,0:T(8,128)}, bf16[4,128,1024]{2,1,0:T(8,128)(2,1)}, bf16[4,128,1024]{2,1...) custom-call(bf16[8,128,1536]{2,1,0:T(8,128)(2,1)} %bitcast.202, bf16[8,128,512]{2,1,0:T(8,128)(2,1)} %bitcast.207, ...), custom_call_target="tpu_custom_call" | custom-call | flops 30000001024 | bytes 16000000 | tf_op jit(solution)/shard_map/reduce_all/pallas_call | solution.py:553
  325.4 1.3 slice.176
  327.5 2.1 convert_reduce_fusion
  336.2 1.2 fusion.57
  (153 shorter events, 34.6 us)
Async XLA Ops:
  7.2 46.0 %all-gather.3.cloned.1.call-start = ((), (), s32[]{:S(2)}) async-start(), calls=%async_computation.1 | async-start | bytes 1179648 | tf_op jit(solution)/shard_map/all_gather | solution.py:809
  7.9 158.3 %all-gather.5.cloned.1.call-start = ((), (), s32[]{:S(2)}) async-start(), calls=%async_computation.2 | async-start | bytes 5308416 | tf_op jit(solution)/shard_map/all_gather | solution.py:811
  53.2 283.0 %reduce-scatter.2.cloned.1.call-start = ((), (), s32[]{:S(2)}) async-start(), calls=%async_computation.3 | async-start | bytes 5308416 | tf_op jit(solution)/shard_map/reduce_scatter | solution.py:871
  108.4 6.4 %copy-start.26 = (bf16[8,128,1536]{2,1,0:T(8,128)(2,1)S(1)}, bf16[8,128,1536]{2,1,0:T(8,128)(2,1)}, u32[]{:S(2)}) copy-start(bf16[8,128,1536]{2,1,0:T(8,128)(2,1)} %get-tuple-element.49) | copy-start | bytes 9437188
  111.1 13.8 %copy-start.10 = (f32[8,16,128]{2,1,0:T(8,128)}, f32[8,16,128]{2,1,0:T(8,128)S(1)}, u32[]{:S(2)}) copy-start(f32[8,16,128]{2,1,0:T(8,128)S(1)} %convert_element_type.110) | copy-start | bytes 196612
  116.6 1.9 copy-start.1
  117.8 1.6 copy-start.5
  117.8 1.9 copy-start.25
  118.6 4.7 %copy-start.20 = (f32[2]{0:T(128)}, f32[2]{0:T(128)S(1)}, u32[]{:S(2)}) copy-start(f32[2]{0:T(128)S(1)} %convert_element_type.117) | copy-start | bytes 28
  119.7 2.1 copy-start.21
  124.9 2.8 copy-start.13
  127.7 17.2 %copy-start.23 = (bf16[1024,512]{1,0:T(8,128)(2,1)S(1)}, bf16[1024,512]{1,0:T(8,128)(2,1)}, u32[]{:S(2)}) copy-start(bf16[1024,512]{1,0:T(8,128)(2,1)} %all-gather.3.cloned.1.call-done) | copy-start | bytes 3145732
  166.2 4.1 %copy-start.28 = (bf16[4,128,1024]{2,1,0:T(8,128)(2,1)S(1)}, bf16[4,128,1024]{2,1,0:T(8,128)(2,1)}, u32[]{:S(2)}) copy-start(bf16[4,128,1024]{2,1,0:T(8,128)(2,1)} %get-tuple-element.55) | copy-start | bytes 3145732
  173.4 1.4 copy-start.33
  173.4 2.0 copy-start.29
  225.6 7.8 %copy-start.3 = (f32[512,512]{1,0:T(8,128)S(1)}, f32[512,512]{1,0:T(8,128)}, u32[]{:S(2)}) copy-start(f32[512,512]{1,0:T(8,128)} %get-tuple-element.61) | copy-start | bytes 3145732
  240.0 4.9 %copy-start.15 = (f32[512,2]{0,1:T(2,128)S(1)}, f32[512,2]{0,1:T(2,128)}, u32[]{:S(2)}) copy-start(f32[512,2]{0,1:T(2,128)} %copy.122) | copy-start | bytes 12292
  240.0 4.9 %copy-start.16 = (f32[512,2]{0,1:T(2,128)S(1)}, f32[512,2]{0,1:T(2,128)}, u32[]{:S(2)}) copy-start(f32[512,2]{0,1:T(2,128)} %copy.121) | copy-start | bytes 12292
  240.0 4.9 %copy-start.7 = (bf16[512,512]{1,0:T(8,128)(2,1)S(1)}, bf16[512,512]{1,0:T(8,128)(2,1)}, u32[]{:S(2)}) copy-start(bf16[512,512]{1,0:T(8,128)(2,1)} %convert_element_type.128) | copy-start | bytes 1572868
  240.0 4.9 %copy-start.27 = (bf16[8,128,1536]{2,1,0:T(8,128)(2,1)S(1)}, bf16[8,128,1536]{2,1,0:T(8,128)(2,1)}, u32[]{:S(2)}) copy-start(bf16[8,128,1536]{2,1,0:T(8,128)(2,1)} %get-tuple-element.49) | copy-start | bytes 9437188
  244.9 1.9 copy-start
  244.9 1.9 copy-start.11
  244.9 1.9 copy-start.17
  249.4 4.3 %copy-start.31 = (bf16[512,768]{1,0:T(8,128)(2,1)S(1)}, bf16[512,768]{1,0:T(8,128)(2,1)}, u32[]{:S(2)}) copy-start(bf16[512,768]{1,0:T(8,128)(2,1)} %copy-done.30) | copy-start | bytes 2359300
  253.7 3.5 copy-start.8
  324.6 5.1 %copy-start.2 = (bf16[128,1024]{1,0:T(8,128)(2,1)S(1)}, bf16[128,1024]{1,0:T(8,128)(2,1)}, u32[]{:S(2)}) copy-start(bf16[128,1024]{1,0:T(8,128)(2,1)} %refs_1_.4) | copy-start | bytes 786436
  324.6 5.1 %copy-start.19 = (f32[128]{0:T(128)S(1)}, f32[128]{0:T(128)}, u32[]{:S(2)}) copy-start(f32[128]{0:T(128)} %add_rsqrt_fusion.1) | copy-start | bytes 1540
  324.6 5.8 %copy-start.14 = (f32[16,128]{1,0:T(8,128)S(1)}, f32[16,128]{1,0:T(8,128)}, u32[]{:S(2)}) copy-start(f32[16,128]{1,0:T(8,128)} %get-tuple-element.71) | copy-start | bytes 24580
  324.6 8.3 %copy-start.4 = (f32[128,1536]{1,0:T(8,128)S(1)}, f32[128,1536]{1,0:T(8,128)}, u32[]{:S(2)}) copy-start(f32[128,1536]{1,0:T(8,128)} %get-tuple-element.69) | copy-start | bytes 2359300
  327.5 6.9 %copy-start.9 = (f32[128,1024]{1,0:T(8,128)S(1)}, f32[128,1024]{1,0:T(8,128)}, u32[]{:S(2)}) copy-start(f32[128,1024]{1,0:T(8,128)} %get-tuple-element.52.refs_3_) | copy-start | bytes 1572868
  329.6 5.5 %copy-start.6 = (f32[128,1024]{1,0:T(8,128)S(1)}, f32[128,1024]{1,0:T(8,128)}, u32[]{:S(2)}) copy-start(f32[128,1024]{1,0:T(8,128)} %get-tuple-element.66) | copy-start | bytes 1572868
  336.2 4.0 %copy-start.12 = (f32[128,512]{1,0:T(8,128)S(1)}, f32[128,512]{1,0:T(8,128)}, u32[]{:S(2)}) copy-start(f32[128,512]{1,0:T(8,128)} %get-tuple-element.253) | copy-start | bytes 786436
  (5 other events, 5.6 us)
Sparse Core Ops, SparseCore 0:
  10.1 42.9 all-gather.2
  55.2 97.1 all-gather.4
  185.1 101.2 reduce-scatter.1
where the time goes:
time: 348 us; the launch traced here: 347 us
  Pallas kernels  192 us (55%)
  waiting for transfers between devices  41.7 us (12%)
  other arithmetic  39 us (11%)
  matrix products  37.1 us (11%)
  local copies, waits for them, and re-layouts  22.7 us (7%)
  between operations  14.3 us (4%)
    pallas_call x1, Pallas kernels, reduce_all(): pl.pallas_call(lambda *refs: reduce_kernel(dp, ranks, lines, count, *refs...  63.9 us
    pallas_call x1, Pallas kernels, gather_all(): pl.pallas_call(lambda *refs: gather_kernel(dp, ranks, widths, count, *ref...  55.2 us
    all_gather x1, waiting for transfers between devices, on_device(): out_full = lax.all_gather(w_out, 'dp', axis=0, tiled=True)  40.9 us
    pallas_call x2, Pallas kernels, turn(): pl.pallas_call(lambda *refs: turn_kernel(ranks, chunks, backward, *refs),...  38.1 us
    pallas_call x1, Pallas kernels, mixer_backward(): pl.pallas_call(lambda *refs: mixer_backward_kernel(heads, key_dim, value_...  18.1 us
    pallas_call x1, Pallas kernels, mixer_forward(): pl.pallas_call(lambda *refs: mixer_forward_kernel(heads, key_dim, value_d...  17.2 us
    dot_general x5, matrix products, times_transpose(): lax.dot_general(left_in, right_in, contract_cols, preferred_element_type=...  13.7 us
    dot_general x5, matrix products, weight_grad(): lax.dot_general(left_in, right_in, contract_rows, preferred_element_type=...  9.81 us
  transfers between devices with their start and end apart: 3, of which 1 were waited for; matrix products, arithmetic and copies ran while one was open for 22% of the time, Pallas kernels for 55%

commit v1 on v0

--- a/solution.py
+++ b/solution.py
@@ -355,9 +355,9 @@
 def gather_kernel(dp, ranks, widths, count, *refs):
     parts = len(widths) + 1
     shards, rows = refs[:parts], refs[parts : parts + count]
-    full_ref, small_ref = refs[parts + count : parts + count + 2]
-    gots = refs[parts + count + 2 : parts + 2 * count + 2]
-    own_sems, ring_sent, ring_got, row_sent, row_got = refs[parts + 2 * count + 2 :]
+    full_ref, last_ref, small_ref = refs[parts + count : parts + count + 3]
+    gots = refs[parts + count + 3 : parts + 2 * count + 3]
+    own_sems, ring_sent, ring_got, row_sent, row_got = refs[parts + 2 * count + 3 :]
     me, mine = lax.axis_index("dp"), lax.axis_index("tensor")
     at, after, before = ring_ends(dp)
     peers = others("tensor")
@@ -369,6 +369,8 @@
     def place(owner, part):
         if part == parts - 1:
             return small_ref.at[owner]
+        if part == parts - 2:
+            return last_ref.at[owner]
         return full_ref.at[owner, :, pl.ds(lefts[part], widths[part])]
 
     flying = {}
@@ -433,9 +435,10 @@
         lambda *refs: gather_kernel(dp, ranks, widths, count, *refs),
         name="gather_all",
         in_specs=[anywhere] * (parts + count),
-        out_specs=[vmem] * (2 + count),
+        out_specs=[vmem] * (3 + count),
         out_shape=[
-            jax.ShapeDtypeStruct((dp, shards[0].shape[0], sum(widths)), shards[0].dtype),
+            jax.ShapeDtypeStruct((dp, shards[0].shape[0], sum(widths[:-1])), shards[0].dtype),
+            jax.ShapeDtypeStruct((dp,) + shards[-1].shape, shards[-1].dtype),
             jax.ShapeDtypeStruct((dp,) + small.shape, small.dtype),
         ]
         + [jax.ShapeDtypeStruct((ranks,) + block.shape, block.dtype) for block in rows],
@@ -451,17 +454,21 @@
             flops=30_000_000_000, bytes_accessed=16_000_000, transcendentals=0
         ),
     )(*shards, small, *rows)
-    full = got[0].reshape(-1, sum(widths))
-    return full, got[1], [block.reshape(-1, block.shape[-1]) for block in got[2:]]
-
-
-def reduce_kernel(dp, ranks, lines, count, *refs):
+    full, last, *blocks = [block.reshape(-1, block.shape[-1]) for block in got[:2] + got[3:]]
+    return full, last, got[2], blocks
+
+
+def reduce_kernel(dp, ranks, lines, count, cuts, *refs):
     arrays = count[0]
     grads, swaps_in, tile_ref = refs[:arrays], refs[arrays : arrays + count[1]], refs[arrays + count[1]]
     refs = refs[arrays + count[1] + 1 :]
-    sums, swaps_out = refs[:arrays], refs[arrays : arrays + count[1]]
-    tiles_ref, lines_ref = refs[arrays + count[1] : arrays + count[1] + 2]
-    refs = refs[arrays + count[1] + 2 :]
+    sums = []
+    for cut in cuts:
+        sums.append(refs[: len(cut)])
+        refs = refs[len(cut) :]
+    swaps_out = refs[: count[1]]
+    tiles_ref, lines_ref = refs[count[1] : count[1] + 2]
+    refs = refs[count[1] + 2 :]
     landed, totals = refs[:arrays], refs[arrays : 2 * arrays]
     ring_sent, ring_got, row_sent, row_got, tile_sent, tile_got, line_sent, line_got = refs[
         2 * arrays :
@@ -520,11 +527,12 @@
                 own, span
             ].astype(jnp.float32)
             if step == last:
-                sums[array][span] = total
+                for (left, width), sum_ref in zip(cuts[array], sums[array]):
+                    sum_ref[span] = total[:, left : left + width]
             else:
                 totals[array][step, span] = total.astype(totals[array].dtype)
                 hop(line, step + 1)
-    small = sums[arrays - 1]
+    small = sums[arrays - 1][0]
     for step, peer in enumerate(peers):
         copies.append(
             send(small, lines_ref.at[mine], line_sent.at[step], line_got.at[step], {"tensor": peer})
@@ -536,7 +544,7 @@
         copy.wait_send()
 
 
-def reduce_all(grads, swaps, tile, number):
+def reduce_all(grads, swaps, tile, number, splits):
     dp, ranks = lax.axis_size("dp"), lax.axis_size("tensor")
     vmem = pl.BlockSpec(memory_space=pltpu.VMEM)
     sem = pltpu.SemaphoreType.DMA
@@ -548,14 +556,22 @@
             lines.append((array, piece * rows // pieces, rows // pieces, piece % 2))
     lines = lines[-2:] + lines[:-2]
     count = (len(grads), len(swaps))
+    cuts = []
+    for widths in splits:
+        cuts.append([(sum(widths[:index]), width) for index, width in enumerate(widths)])
+    pieces = [
+        jax.ShapeDtypeStruct((grad.shape[1], width), jnp.float32)
+        for grad, widths in zip(grads, splits)
+        for width in widths
+    ]
     inputs = list(grads) + list(swaps) + [tile]
     small = grads[-1].shape[1:]
     results = pl.pallas_call(
-        lambda *refs: reduce_kernel(dp, ranks, lines, count, *refs),
+        lambda *refs: reduce_kernel(dp, ranks, lines, count, cuts, *refs),
         name="reduce_all",
         in_specs=[vmem] * len(inputs),
-        out_specs=[vmem] * (len(inputs) + 1),
-        out_shape=[jax.ShapeDtypeStruct(grad.shape[1:], jnp.float32) for grad in grads]
+        out_specs=[vmem] * (len(pieces) + len(swaps) + 2),
+        out_shape=pieces
         + [jax.ShapeDtypeStruct(block.shape, block.dtype) for block in swaps]
         + [
             jax.ShapeDtypeStruct((dp,) + tile.shape, tile.dtype),
@@ -578,7 +594,7 @@
             flops=30_000_000_000, bytes_accessed=16_000_000, transcendentals=0
         ),
     )(*inputs)
-    arrays = len(grads)
+    arrays = len(pieces)
     return results[:arrays], results[arrays : arrays + len(swaps)], results[-2], results[-1]
 
 
@@ -806,11 +822,9 @@
         bf16,
     )[0]
     ffn_pack = jnp.concatenate([pad_columns(w, ff) for w in (w_up_gate, w_up, w_down)], axis=1)
-    out_full = lax.all_gather(w_out, "dp", axis=0, tiled=True)
-    out_full, ffn_pack = lax.optimization_barrier((out_full, ffn_pack))
     ffn_full = lax.all_gather(ffn_pack, "dp", axis=0, tiled=True)
-    in_full, small_full, (tokens_got, cot_full) = gather_all(
-        [w_query, w_key, w_value, w_gate_out], small, [tokens, cotangent], 1
+    in_full, out_full, small_full, (tokens_got, cot_full) = gather_all(
+        [w_query, w_key, w_value, w_gate_out, w_out], small, [tokens, cotangent], 1
     )
     small_all = small_full.astype(f32)
 
@@ -914,8 +928,9 @@
         ],
         rate_tile,
         7,
-    )
-    in_sums, out_sums, small_sums = sums
+        [[qk_width, qk_width, v_width, v_width], [v_width], [small_width]],
+    )
+    query_sums, key_sums, value_sums, gate_sums, out_sums, small_sums = sums
     grad_normed_one = jnp.sum(swapped[0].astype(f32), axis=0)
     result = (middle + jnp.sum(swapped[1].astype(f32), axis=0)).astype(bf16)
     grad_rows = grad_middle + norm_backward(grad_normed_one, unit_one, scale_one, gain_one)
@@ -934,10 +949,10 @@
         result,
         grad_rows,
         gain_sums[0],
-        in_sums[:, :qk_width],
-        in_sums[:, qk_width : 2 * qk_width],
-        in_sums[:, 2 * qk_width : conv_width],
-        in_sums[:, conv_width:],
+        query_sums,
+        key_sums,
+        value_sums,
+        gate_sums,
         out_sums,
         lines_out(2),
         lines_out(2 + heads),

time: 348 us -> 342 us (0.983)
  waiting for transfers between devices: 41.7 us -> 0.06 us
  Pallas kernels: 192 us -> 226 us
    all_gather x1 -> x0, waiting for transfers between devices: 40.9 us -> none  [on_device(): out_full = lax.all_gather(w_out, 'dp', axis=0, tiled=True)]
    pallas_call x1, Pallas kernels: 55.2 us -> 81.7 us  [gather_all(): pl.pallas_call(lambda *refs: gather_kernel(dp, ranks, widths, count, *ref...]
    pallas_call x1, Pallas kernels: 63.9 us -> 70.1 us  [reduce_all(): pl.pallas_call(lambda *refs: reduce_kernel(dp, ranks, lines, count, cuts,...]
    unnamed x74 -> x86, local copies, waits for them, and re-layouts: 5.14 us -> 7.88 us
  transfers between devices with their start and end apart: 3 -> 2, of which waited for: 1 -> 0; matrix products, arithmetic and copies ran while one was open for 22% -> 21% of each run, Pallas kernels for 55% -> 66%
where the time goes in v1:
time: 342 us; the launch traced here: 341 us
  Pallas kernels  226 us (66%)
  other arithmetic  38.8 us (11%)
  matrix products  37.1 us (11%)
  local copies, waits for them, and re-layouts  24.4 us (7%)
  between operations  14.6 us (4%)
    pallas_call x1, Pallas kernels, gather_all(): pl.pallas_call(lambda *refs: gather_kernel(dp, ranks, widths, count, *ref...  81.7 us
    pallas_call x1, Pallas kernels, reduce_all(): pl.pallas_call(lambda *refs: reduce_kernel(dp, ranks, lines, count, cuts,...  70.1 us
    pallas_call x2, Pallas kernels, turn(): pl.pallas_call(lambda *refs: turn_kernel(ranks, chunks, backward, *refs),...  38.5 us
    pallas_call x1, Pallas kernels, mixer_backward(): pl.pallas_call(lambda *refs: mixer_backward_kernel(heads, key_dim, value_...  18.2 us
    pallas_call x1, Pallas kernels, mixer_forward(): pl.pallas_call(lambda *refs: mixer_forward_kernel(heads, key_dim, value_d...  17.2 us
    dot_general x5, matrix products, times_transpose(): lax.dot_general(left_in, right_in, contract_cols, preferred_element_type=...  13.7 us
    dot_general x5, matrix products, weight_grad(): lax.dot_general(left_in, right_in, contract_rows, preferred_element_type=...  9.77 us
    unnamed x86, local copies, waits for them, and re-layouts  7.88 us
  transfers between devices with their start and end apart: 2, of which 0 were waited for; matrix products, arithmetic and copies ran while one was open for 21% of the time, Pallas kernels for 66%

profile of v1, /device:TPU:0, one launch (start us, length us, event | category | flops | bytes accessed | tf_op | source)
XLA Modules:
  0.0 340.6 jit_solution(17990955964260361498)
XLA Ops:
  7.2 1.9 fusion.19
  11.5 81.7 %gather_all.1 = (bf16[8,128,1536]{2,1,0:T(8,128)(2,1)}, bf16[8,128,512]{2,1,0:T(8,128)(2,1)}, bf16[8,16,128]{2,1,0:T(8,128)(2,1)}, bf16[4,128,1024]{2,1,0:T(8,128)(2,1)}, bf16[4,128,1024]{2,1,0:T(8,128)(2,1)}) custom-call(bf16[128,256]{1,0:T(8,128)(2,1)} %refs_0_.1, bf16[128,256]{1,0:T(8,128)(2,1)} %refs_1_.3, bf16[128,512]{1,0:T(8,128)(2,1)} %refs_2_.1, ...), custom_call_target="tpu_custom_call" | custom-call | flops 30000001024 | bytes 16000000 | tf_op jit(solution)/shard_map/gather_all/pallas_call | solution.py:434
  95.8 1.5 multiply_reduce_fusion.5
  97.9 1.5 multiply_convert_fusion.1
  99.4 1.8 fusion.59
  101.3 1.1 slice.179.refs_1_
  107.9 1.1 fusion.24
  110.2 2.2 multiply_add_fusion.refs_0_
  112.4 17.2 %mixer_forward.1 = (bf16[512,512]{1,0:T(8,128)(2,1)}, f32[4,2,128,256]{3,2,1,0:T(8,128)}, f32[4,2,128,128]{3,2,1,0:T(8,128)}) custom-call(f32[512,1024]{1,0:T(8,128)} %multiply_add_fusion.refs_0_, f32[512,512]{1,0:T(8,128)} %slice.179.refs_1_, f32[512,4]{1,0:T(8,128)} %pad_maximum_fusion.7.refs_2_, f32[1,512]{1,0:T(1,128)} %reshape.235.refs_3_), custom_call_target="tpu_custom_call" | custom-call | flops 30000001024 | bytes 8000000 | tf_op jit(solution)/shard_map/mixer_forward/pallas_call | solution.py:239
  129.6 2.8 convolution_convert_fusion.5
  132.4 18.9 %turn_forward.1 = (bf16[4,128,1024]{2,1,0:T(8,128)(2,1)}, f32[128,1024]{1,0:T(8,128)}) custom-call(bf16[4,128,1024]{2,1,0:T(8,128)(2,1)} %bitcast.215, bf16[128,1024]{1,0:T(8,128)(2,1)} %refs_1_.4, f32[1,1024]{1,0:T(1,128)} %slice_bitcast_fusion.1.refs_2_), custom_call_target="tpu_custom_call" | custom-call | flops 10000000000 | bytes 4000000 | tf_op jit(solution)/shard_map/turn_forward/pallas_call | solution.py:723
  151.4 4.1 %fusion.2 = f32[512,1536]{1,0:T(8,128)S(1)} fusion(bf16[512,1024]{1,0:T(8,128)(2,1)} %bitcast.212, bf16[1024,2304]{0,1:T(8,128)(2,1)} %all-gather.2.cloned.1.call-done), kind=kOutput, calls=%fused_computation.5 | convolution fusion | flops 1610612736 | bytes 7340032 | tf_op jit(solution)/shard_map/dot_general | solution.py:867
  155.5 3.0 multiply_convert_fusion.4
  160.5 1.8 convolution_convert_fusion.1
  162.4 2.4 pad_maximum_fusion
  164.8 5.2 %fusion.5 = bf16[512,1024]{1,0:T(8,128)(2,1)} fusion(bf16[1024,2304]{0,1:T(8,128)(2,1)} %all-gather.2.cloned.1.call-done, bf16[512,768]{1,0:T(8,128)(2,1)} %copy-done.37, bf16[512,768]{1,0:T(8,128)(2,1)} %copy-done.36), kind=kOutput, calls=%fused_computation.36 | convolution fusion | flops 1614282752 | bytes 5767168 | tf_op jit(solution)/shard_map/dot_general | solution.py:34
  170.0 19.5 %turn_backward.1 = (bf16[4,128,1024]{2,1,0:T(8,128)(2,1)}, f32[128,1024]{1,0:T(8,128)}, f32[1,1024]{1,0:T(1,128)}) custom-call(bf16[4,128,1024]{2,1,0:T(8,128)(2,1)} %bitcast.214, bf16[128,1024]{1,0:T(8,128)(2,1)} %refs_1_.5, f32[1,1024]{1,0:T(1,128)} %slice_bitcast_fusion.1.refs_2_, f32[128,1024]{1,0:T(8,128)} %get-tuple-element.54.refs_3_), custom_call_target="tpu_custom_call" | custom-call | flops 10000000000 | bytes 4000000 | tf_op jit(solution)/shard_map/turn_backward/pallas_call | solution.py:723
  189.5 3.0 fusion.60.refs_6_
  192.5 18.2 %mixer_backward.1 = (f32[512,1024]{1,0:T(8,128)}, f32[512,512]{1,0:T(8,128)}, f32[512,4]{1,0:T(8,128)}, f32[1,512]{1,0:T(1,128)}) custom-call(f32[512,1024]{1,0:T(8,128)} %multiply_add_fusion.refs_0_, f32[512,512]{1,0:T(8,128)} %slice.179.refs_1_, f32[512,4]{1,0:T(8,128)} %pad_maximum_fusion.7.refs_2_, f32[1,512]{1,0:T(1,128)} %reshape.235.refs_3_, ...), custom_call_target="tpu_custom_call" | custom-call | flops 30000001024 | bytes 12000000 | tf_op jit(solution)/shard_map/mixer_backward/pallas_call | solution.py:273
  211.2 1.3 reduce.4
  213.2 2.6 fusion.52
  219.9 5.4 %multiply_reduce_fusion.3 = (f32[1024]{0:T(1024)S(1)}, f32[1024]{0:T(1024)S(1)}, f32[1024]{0:T(1024)S(1)}, f32[1024]{0:T(1024)S(1)}, f32[512,1024]{1,0:T(8,128)}...) fusion(f32[512,1024]{1,0:T(8,128)} %get-tuple-element.61, f32[512,1024]{1,0:T(8,128)S(1)} %slice.171, ...), kind=kLoop, calls=%fused_computation.17 | loop fusion | flops 6287360 | bytes 14712832 | tf_op jit(solution)/shard_map/transpose(jvp())/reduce_sum | solution.py:749
  225.6 4.7 %fusion.4 = bf16[512,1024]{1,0:T(8,128)(2,1)S(1)} fusion(f32[512,1024]{1,0:T(8,128)} %get-tuple-element.189, f32[512,1024]{1,0:T(8,128)} %get-tuple-element.190, f32[512,1024]{1,0:T(8,128)} %get-tuple-element.191, f32[512,1024]{1,0:T(8,128)} %get-tuple-element.192), kind=kLoop, calls=%fused_computation.8 | loop fusion | flops 2097152 | bytes 9437184 | tf_op jit(solution)/shard_map/convert.3
  230.4 1.8 fusion.15
  232.3 1.8 fusion.54
  236.1 3.1 convolution_convert_fusion.4
  239.2 3.5 %convolution_convert_fusion.3 = bf16[512,1024]{1,0:T(8,128)(2,1)} fusion(bf16[512,768]{1,0:T(8,128)(2,1)S(1)} %copy-done.35, bf16[1024,2304]{0,1:T(8,128)(2,1)} %all-gather.2.cloned.1.call-done), kind=kOutput, calls=%fused_computation.35 | convolution fusion | flops 805830656 | bytes 3407872 | tf_op jit(solution)/shard_map/dot_general | solution.py:34
  242.7 3.5 %convolution_convert_fusion = bf16[1024,1536]{1,0:T(8,128)(2,1)} fusion(bf16[512,1024]{1,0:T(8,128)(2,1)S(1)} %get-tuple-element.193, bf16[512,512]{1,0:T(8,128)(2,1)S(1)} %copy-done.7, bf16[512,1024]{1,0:T(8,128)(2,1)S(1)} %fusion.4), kind=kOutput, calls=%fused_computation.1 | convolution fusion | flops 1615331328 | bytes 5767168 | tf_op jit(solution)/shard_map/dot_general | solution.py:30
  246.1 70.1 %reduce_all.1 = (f32[128,256]{1,0:T(8,128)}, f32[128,256]{1,0:T(8,128)}, f32[128,512]{1,0:T(8,128)}, f32[128,512]{1,0:T(8,128)}, f32[128,512]{1,0:T(8,128)}, /*i...) custom-call(bf16[8,128,1536]{2,1,0:T(8,128)(2,1)} %bitcast.203, ...), custom_call_target="tpu_custom_call" | custom-call | flops 30000001024 | bytes 16000000 | tf_op jit(solution)/shard_map/reduce_all/pallas_call | solution.py:569
  317.1 1.3 slice.160
  319.2 2.1 convert_reduce_fusion
  326.4 1.3 fusion.55
  (160 shorter events, 34.5 us)
Async XLA Ops:
  7.2 144.1 %all-gather.2.cloned.1.call-start = ((), (), s32[]{:S(2)}) async-start(), calls=%async_computation.1 | async-start | bytes 5308416 | tf_op jit(solution)/shard_map/all_gather | solution.py:825
  9.2 317.2 %reduce-scatter.2.cloned.1.call-start = ((), (), s32[]{:S(2)}) async-start(), calls=%async_computation.2 | async-start | bytes 5308416 | tf_op jit(solution)/shard_map/reduce_scatter | solution.py:885
  93.2 6.2 %copy-start.29 = (bf16[8,128,1536]{2,1,0:T(8,128)(2,1)S(1)}, bf16[8,128,1536]{2,1,0:T(8,128)(2,1)}, u32[]{:S(2)}) copy-start(bf16[8,128,1536]{2,1,0:T(8,128)(2,1)} %get-tuple-element.51) | copy-start | bytes 9437188
  95.8 13.8 %copy-start.9 = (f32[8,16,128]{2,1,0:T(8,128)}, f32[8,16,128]{2,1,0:T(8,128)S(1)}, u32[]{:S(2)}) copy-start(f32[8,16,128]{2,1,0:T(8,128)S(1)} %convert_element_type.110) | copy-start | bytes 196612
  101.2 2.0 copy-start.1
  102.4 1.9 copy-start.28
  103.2 4.7 %copy-start.24 = (f32[2]{0:T(128)}, f32[2]{0:T(128)S(1)}, u32[]{:S(2)}) copy-start(f32[2]{0:T(128)S(1)} %convert_element_type.117) | copy-start | bytes 28
  104.3 2.1 copy-start.25
  109.6 2.8 copy-start.16
  112.4 17.2 %copy-start.31 = (bf16[8,128,512]{2,1,0:T(8,128)(2,1)S(1)}, bf16[8,128,512]{2,1,0:T(8,128)(2,1)}, u32[]{:S(2)}) copy-start(bf16[8,128,512]{2,1,0:T(8,128)(2,1)} %get-tuple-element.53) | copy-start | bytes 3145732
  151.3 4.1 %copy-start.32 = (bf16[4,128,1024]{2,1,0:T(8,128)(2,1)S(1)}, bf16[4,128,1024]{2,1,0:T(8,128)(2,1)}, u32[]{:S(2)}) copy-start(bf16[4,128,1024]{2,1,0:T(8,128)(2,1)} %get-tuple-element.57) | copy-start | bytes 3145732
  158.5 2.0 copy-start.33
  210.7 8.3 %copy-start.3 = (f32[512,512]{1,0:T(8,128)S(1)}, f32[512,512]{1,0:T(8,128)}, u32[]{:S(2)}) copy-start(f32[512,512]{1,0:T(8,128)} %get-tuple-element.62) | copy-start | bytes 3145732
  225.6 4.7 %copy-start.19 = (f32[512,2]{0,1:T(2,128)S(1)}, f32[512,2]{0,1:T(2,128)}, u32[]{:S(2)}) copy-start(f32[512,2]{0,1:T(2,128)} %copy.122) | copy-start | bytes 12292
  225.6 4.7 %copy-start.20 = (f32[512,2]{0,1:T(2,128)S(1)}, f32[512,2]{0,1:T(2,128)}, u32[]{:S(2)}) copy-start(f32[512,2]{0,1:T(2,128)} %copy.121) | copy-start | bytes 12292
  225.6 4.7 %copy-start.6 = (bf16[512,512]{1,0:T(8,128)(2,1)S(1)}, bf16[512,512]{1,0:T(8,128)(2,1)}, u32[]{:S(2)}) copy-start(bf16[512,512]{1,0:T(8,128)(2,1)} %convert_element_type.128) | copy-start | bytes 1572868
  225.6 4.7 %copy-start.30 = (bf16[8,128,1536]{2,1,0:T(8,128)(2,1)S(1)}, bf16[8,128,1536]{2,1,0:T(8,128)(2,1)}, u32[]{:S(2)}) copy-start(bf16[8,128,1536]{2,1,0:T(8,128)(2,1)} %get-tuple-element.51) | copy-start | bytes 9437188
  230.4 1.9 copy-start
  230.4 1.9 copy-start.10
  230.4 1.9 copy-start.21
  234.8 4.3 %copy-start.35 = (bf16[512,768]{1,0:T(8,128)(2,1)S(1)}, bf16[512,768]{1,0:T(8,128)(2,1)}, u32[]{:S(2)}) copy-start(bf16[512,768]{1,0:T(8,128)(2,1)} %copy-done.34) | copy-start | bytes 2359300
  239.2 3.5 %copy-start.7 = (bf16[512,512]{1,0:T(8,128)(2,1)S(1)}, bf16[512,512]{1,0:T(8,128)(2,1)}, u32[]{:S(2)}) copy-start(bf16[512,512]{1,0:T(8,128)(2,1)} %convert_element_type.128) | copy-start | bytes 1572868
  316.2 5.1 %copy-start.2 = (bf16[128,1024]{1,0:T(8,128)(2,1)S(1)}, bf16[128,1024]{1,0:T(8,128)(2,1)}, u32[]{:S(2)}) copy-start(bf16[128,1024]{1,0:T(8,128)(2,1)} %refs_1_.4) | copy-start | bytes 786436
  316.3 5.1 %copy-start.23 = (f32[128]{0:T(128)S(1)}, f32[128]{0:T(128)}, u32[]{:S(2)}) copy-start(f32[128]{0:T(128)} %add_rsqrt_fusion.1) | copy-start | bytes 1540
  316.3 5.8 %copy-start.18 = (f32[16,128]{1,0:T(8,128)S(1)}, f32[16,128]{1,0:T(8,128)}, u32[]{:S(2)}) copy-start(f32[16,128]{1,0:T(8,128)} %get-tuple-element.75) | copy-start | bytes 24580
  316.3 8.3 %copy-start.8 = (f32[128,1024]{1,0:T(8,128)S(1)}, f32[128,1024]{1,0:T(8,128)}, u32[]{:S(2)}) copy-start(f32[128,1024]{1,0:T(8,128)} %get-tuple-element.54.refs_3_) | copy-start | bytes 1572868
  319.2 6.1 %copy-start.5 = (f32[128,1024]{1,0:T(8,128)S(1)}, f32[128,1024]{1,0:T(8,128)}, u32[]{:S(2)}) copy-start(f32[128,1024]{1,0:T(8,128)} %get-tuple-element.67) | copy-start | bytes 1572868
  326.4 4.0 %copy-start.15 = (f32[128,256]{1,0:T(8,128)S(1)}, f32[128,256]{1,0:T(8,128)}, u32[]{:S(2)}) copy-start(f32[128,256]{1,0:T(8,128)} %get-tuple-element.249) | copy-start | bytes 393220
  326.4 4.7 %copy-start.14 = (f32[128,256]{1,0:T(8,128)S(1)}, f32[128,256]{1,0:T(8,128)}, u32[]{:S(2)}) copy-start(f32[128,256]{1,0:T(8,128)} %get-tuple-element.250) | copy-start | bytes 393220
  326.4 5.3 %copy-start.13 = (f32[128,512]{1,0:T(8,128)S(1)}, f32[128,512]{1,0:T(8,128)}, u32[]{:S(2)}) copy-start(f32[128,512]{1,0:T(8,128)} %get-tuple-element.251) | copy-start | bytes 786436
  327.6 4.8 %copy-start.12 = (f32[128,512]{1,0:T(8,128)S(1)}, f32[128,512]{1,0:T(8,128)}, u32[]{:S(2)}) copy-start(f32[128,512]{1,0:T(8,128)} %get-tuple-element.252) | copy-start | bytes 786436
  327.6 5.5 %copy-start.11 = (f32[128,512]{1,0:T(8,128)S(1)}, f32[128,512]{1,0:T(8,128)}, u32[]{:S(2)}) copy-start(f32[128,512]{1,0:T(8,128)} %get-tuple-element.253) | copy-start | bytes 786436
  (8 other events, 9.9 us)
Sparse Core Ops, SparseCore 0:
  10.0 107.5 all-gather.1
  170.1 107.2 reduce-scatter.1

commit v2 on v1

--- a/solution.py
+++ b/solution.py
@@ -822,10 +822,12 @@
         bf16,
     )[0]
     ffn_pack = jnp.concatenate([pad_columns(w, ff) for w in (w_up_gate, w_up, w_down)], axis=1)
+    qk_full, value_full, small_full, (tokens_got,) = gather_all(
+        [w_query, w_key, w_value], small, [tokens], 1
+    )
+    small_full, ffn_pack, gate_in = lax.optimization_barrier((small_full, ffn_pack, w_gate_out))
     ffn_full = lax.all_gather(ffn_pack, "dp", axis=0, tiled=True)
-    in_full, out_full, small_full, (tokens_got, cot_full) = gather_all(
-        [w_query, w_key, w_value, w_gate_out, w_out], small, [tokens, cotangent], 1
-    )
+    gate_full, out_full, _, (cot_full,) = gather_all([gate_in, w_out], small, [cotangent], 2)
     small_all = small_full.astype(f32)
 
     def group_of(index, rows):
@@ -845,10 +847,13 @@
     tokens_full = tokens_got.astype(f32)
     _, unit_full = norm_forward(tokens_full)
     normed_one = (unit_full * gain_one).astype(bf16)
-    projected = jnp.dot(normed_one, in_full, preferred_element_type=f32)
+    in_parts = (qk_full, value_full, gate_full)
+    in_edges = (0, 2 * qk_width, conv_width, in_width)
+    proj_qk, proj_value, proj_gate = [
+        jnp.dot(normed_one, part, preferred_element_type=f32) for part in in_parts
+    ]
     proj_rates = times_transpose(normed_one, rate_weights)
-    proj_conv = projected[:, :conv_width]
-    proj_gate = projected[:, conv_width:]
+    proj_conv = jnp.concatenate([proj_qk, proj_value], axis=1)
     conv_all, conv_pull = jax.vjp(short_conv, proj_conv, conv_weights)
     rates, rates_pull = jax.vjp(
         rate_terms, proj_rates[:, :heads], proj_rates[:, heads:], a_log.astype(f32),
@@ -860,7 +865,7 @@
     row_values = tokens.astype(f32)
     scale_one, unit_one = norm_forward(row_values)
     normed_two, middle = turn(
-        times_transpose(mixed, out_full).astype(bf16), tokens, gain_two, 2
+        times_transpose(mixed, out_full).astype(bf16), tokens, gain_two, 4
     )
     gates_full, down_full = ffn_full[:, : 2 * ff], ffn_full[:, 2 * ff :]
     grad_hidden = jnp.dot(cot_full, down_full, preferred_element_type=f32)
@@ -899,9 +904,10 @@
     grad_beta, grad_alpha, grad_rate_part, grad_bias_part = rates_pull(grad_rates)
     grad_proj = jnp.concatenate([grad_pconv.astype(bf16), grad_pgate.astype(bf16)], axis=1)
     grad_rate_proj = jnp.concatenate([grad_beta, grad_alpha], axis=1).astype(bf16)
-    grad_normed_part = times_transpose(grad_proj, in_full) + jnp.dot(
-        grad_rate_proj, rate_weights, preferred_element_type=f32
-    )
+    grad_normed_part = jnp.dot(grad_rate_proj, rate_weights, preferred_element_type=f32)
+    for index, part in enumerate(in_parts):
+        left, right = in_edges[index : index + 2]
+        grad_normed_part = grad_normed_part + times_transpose(grad_proj[:, left:right], part)
     grad_gain_one = jnp.sum(grad_normed_part * unit_full, axis=0)
     grad_lines = jnp.concatenate(
         [grad_gain_one[None], grad_gain_two, weight_grad(grad_rate_proj, normed_one)], axis=0

time: 342 us -> 332 us (0.971)
  Pallas kernels: 226 us -> 210 us
  matrix products: 37.1 us -> 42.3 us
    pallas_call x1 -> x2, Pallas kernels: 81.7 us -> 71.1 us  [gather_all(): pl.pallas_call(lambda *refs: gather_kernel(dp, ranks, widths, count, *ref...]
    pallas_call x1, Pallas kernels: 70.1 us -> 64.4 us  [reduce_all(): pl.pallas_call(lambda *refs: reduce_kernel(dp, ranks, lines, count, cuts,...]
    dot_general x1 -> x3, matrix products: 1.81 us -> 5.87 us  [on_device(): jnp.dot(normed_one, part, preferred_element_type=f32)]
    dot_general x5 -> x7, matrix products: 13.7 us -> 15.8 us  [times_transpose(): lax.dot_general(left_in, right_in, contract_cols, preferred_element_type=...]
    unnamed x86 -> x94, local copies, waits for them, and re-layouts: 7.88 us -> 8.78 us
  transfers between devices with their start and end apart: 2 -> 2, of which waited for: 0 -> 0; matrix products, arithmetic and copies ran while one was open for 21% -> 22% of each run, Pallas kernels for 66% -> 54%
where the time goes in v2:
time: 332 us; the launch traced here: 331 us
  Pallas kernels  210 us (63%)
  matrix products  42.3 us (13%)
  other arithmetic  37.6 us (11%)
  local copies, waits for them, and re-layouts  26 us (8%)
  between operations  14.7 us (4%)
    pallas_call x2, Pallas kernels, gather_all(): pl.pallas_call(lambda *refs: gather_kernel(dp, ranks, widths, count, *ref...  71.1 us
    pallas_call x1, Pallas kernels, reduce_all(): pl.pallas_call(lambda *refs: reduce_kernel(dp, ranks, lines, count, cuts,...  64.4 us
    pallas_call x2, Pallas kernels, turn(): pl.pallas_call(lambda *refs: turn_kernel(ranks, chunks, backward, *refs),...  39.9 us
    pallas_call x1, Pallas kernels, mixer_backward(): pl.pallas_call(lambda *refs: mixer_backward_kernel(heads, key_dim, value_...  18.1 us
    pallas_call x1, Pallas kernels, mixer_forward(): pl.pallas_call(lambda *refs: mixer_forward_kernel(heads, key_dim, value_d...  16.9 us
    dot_general x7, matrix products, times_transpose(): lax.dot_general(left_in, right_in, contract_cols, preferred_element_type=...  15.8 us
    dot_general x5, matrix products, weight_grad(): lax.dot_general(left_in, right_in, contract_rows, preferred_element_type=...  9.8 us
    unnamed x94, local copies, waits for them, and re-layouts  8.78 us
  transfers between devices with their start and end apart: 2, of which 0 were waited for; matrix products, arithmetic and copies ran while one was open for 22% of the time, Pallas kernels for 54%

profile of v2, /device:TPU:0, one launch (start us, length us, event | category | flops | bytes accessed | tf_op | source)
XLA Modules:
  0.0 331.1 jit_solution(2366122957499095679)
XLA Ops:
  9.5 2.0 fusion.20
  11.5 30.6 %gather_all.2 = (bf16[8,128,512]{2,1,0:T(8,128)(2,1)}, bf16[8,128,512]{2,1,0:T(8,128)(2,1)}, bf16[8,16,128]{2,1,0:T(8,128)(2,1)}, bf16[4,128,1024]{2,1,0:T(8,128)(2,1)}) custom-call(bf16[128,256]{1,0:T(8,128)(2,1)} %refs_0_.1, bf16[128,256]{1,0:T(8,128)(2,1)} %refs_1_.4, bf16[128,512]{1,0:T(8,128)(2,1)} %refs_2_.1, bf16[16,128]{1,0:T(8,128)(2,1)} %fusion.41.refs_3_.refs_2_, ...), custom_call_target="tpu_custom_call" | custom-call | flops 30000001024 | bytes 16000000 | tf_op jit(solution)/shard_map/gather_all/pallas_call | solution.py:434
  45.6 1.5 multiply_reduce_fusion.5
  52.1 1.9 fusion.65
  56.9 40.5 %gather_all.3 = (bf16[8,128,512]{2,1,0:T(8,128)(2,1)}, bf16[8,128,512]{2,1,0:T(8,128)(2,1)}, bf16[8,16,128]{2,1,0:T(8,128)(2,1)}, bf16[4,128,1024]{2,1,0:T(8,128)(2,1)}) custom-call(bf16[128,512]{1,0:T(8,128)(2,1)} %refs_0_.2, bf16[128,512]{1,0:T(8,128)(2,1)} %refs_1_.5, bf16[16,128]{1,0:T(8,128)(2,1)} %fusion.41.refs_3_.refs_2_, bf16[128,1024]{1,0:T(8,128)(2,1)} %refs_1_.7), custom_call_target="tpu_custom_call" | custom-call | flops 30000001024 | bytes 16000000 | tf_op jit(solution)/shard_map/gather_all/pallas_call | solution.py:434
  97.4 3.2 fusion.66.refs_1_
  100.6 2.2 multiply_add_fusion.refs_0_
  102.8 16.9 %mixer_forward.1 = (bf16[512,512]{1,0:T(8,128)(2,1)}, f32[4,2,128,256]{3,2,1,0:T(8,128)}, f32[4,2,128,128]{3,2,1,0:T(8,128)}) custom-call(f32[512,1024]{1,0:T(8,128)} %multiply_add_fusion.refs_0_, f32[512,512]{1,0:T(8,128)} %fusion.66.refs_1_, f32[512,4]{1,0:T(8,128)} %pad_maximum_fusion.5.refs_2_, f32[1,512]{1,0:T(1,128)} %reshape.265.refs_3_), custom_call_target="tpu_custom_call" | custom-call | flops 30000001024 | bytes 8000000 | tf_op jit(solution)/shard_map/mixer_forward/pallas_call | solution.py:239
  119.7 3.1 convolution_convert_fusion.5
  122.8 20.3 %turn_forward.1 = (bf16[4,128,1024]{2,1,0:T(8,128)(2,1)}, f32[128,1024]{1,0:T(8,128)}) custom-call(bf16[4,128,1024]{2,1,0:T(8,128)(2,1)} %bitcast.228, bf16[128,1024]{1,0:T(8,128)(2,1)} %refs_1_.6, f32[1,1024]{1,0:T(1,128)} %slice_bitcast_fusion.1.refs_2_), custom_call_target="tpu_custom_call" | custom-call | flops 10000000000 | bytes 4000000 | tf_op jit(solution)/shard_map/turn_forward/pallas_call | solution.py:723
  143.1 4.1 %fusion.2 = f32[512,1536]{1,0:T(8,128)S(1)} fusion(bf16[512,1024]{1,0:T(8,128)(2,1)} %bitcast.225, bf16[1024,2304]{0,1:T(8,128)(2,1)} %all-gather.2.cloned.1.call-done), kind=kOutput, calls=%fused_computation.5 | convolution fusion | flops 1610612736 | bytes 7340032 | tf_op jit(solution)/shard_map/dot_general | solution.py:872
  147.2 3.0 multiply_convert_fusion.4
  152.3 1.8 convolution_convert_fusion.1
  154.1 2.5 pad_maximum_fusion
  156.6 5.2 %fusion.7 = bf16[512,1024]{1,0:T(8,128)(2,1)} fusion(bf16[1024,2304]{0,1:T(8,128)(2,1)} %all-gather.2.cloned.1.call-done, bf16[512,768]{1,0:T(8,128)(2,1)} %copy-done.41, bf16[512,768]{1,0:T(8,128)(2,1)} %copy-done.40), kind=kOutput, calls=%fused_computation.36 | convolution fusion | flops 1614282752 | bytes 5767168 | tf_op jit(solution)/shard_map/dot_general | solution.py:34
  161.9 19.6 %turn_backward.1 = (bf16[4,128,1024]{2,1,0:T(8,128)(2,1)}, f32[128,1024]{1,0:T(8,128)}, f32[1,1024]{1,0:T(1,128)}) custom-call(bf16[4,128,1024]{2,1,0:T(8,128)(2,1)} %bitcast.227, bf16[128,1024]{1,0:T(8,128)(2,1)} %refs_1_.7, f32[1,1024]{1,0:T(1,128)} %slice_bitcast_fusion.1.refs_2_, f32[128,1024]{1,0:T(8,128)} %get-tuple-element.63.refs_3_), custom_call_target="tpu_custom_call" | custom-call | flops 10000000000 | bytes 4000000 | tf_op jit(solution)/shard_map/turn_backward/pallas_call | solution.py:723
  181.4 3.3 fusion.67.refs_6_
  184.7 18.1 %mixer_backward.1 = (f32[512,1024]{1,0:T(8,128)}, f32[512,512]{1,0:T(8,128)}, f32[512,4]{1,0:T(8,128)}, f32[1,512]{1,0:T(1,128)}) custom-call(f32[512,1024]{1,0:T(8,128)} %multiply_add_fusion.refs_0_, f32[512,512]{1,0:T(8,128)} %fusion.66.refs_1_, f32[512,4]{1,0:T(8,128)} %pad_maximum_fusion.5.refs_2_, f32[1,512]{1,0:T(1,128)} %reshape.265.refs_3_, ...), custom_call_target="tpu_custom_call" | custom-call | flops 30000001024 | bytes 12000000 | tf_op jit(solution)/shard_map/mixer_backward/pallas_call | solution.py:273
  203.4 1.3 reduce.4
  205.4 2.6 fusion.57
  211.2 2.2 convert_element_type.132
  213.4 4.9 %multiply_reduce_fusion.3 = (f32[1024]{0:T(1024)S(1)}, f32[1024]{0:T(1024)S(1)}, f32[1024]{0:T(1024)S(1)}, f32[1024]{0:T(1024)S(1)}, f32[512,1024]{1,0:T(8,128)}...) fusion(f32[512,1024]{1,0:T(8,128)} %get-tuple-element.71, f32[512,1024]{1,0:T(8,128)S(1)} %pad_maximum_fusion.1, ...), kind=kLoop, calls=%fused_computation.16 | loop fusion | flops 6811648 | bytes 14712832 | tf_op jit(solution)/shard_map/transpose(jvp())/reduce_sum | solution.py:749
  218.6 4.6 %add_convert_fusion = bf16[515,1024]{1,0:T(8,128)(2,1)S(1)} fusion(f32[512,1024]{1,0:T(8,128)} %get-tuple-element.199, f32[512,1024]{1,0:T(8,128)} %get-tuple-element.200, f32[512,1024]{1,0:T(8,128)} %get-tuple-element.201, f32[512,1024]{1,0:T(8,128)} %get-tuple-element.202), kind=kLoop, calls=%fused_computation.7 | loop fusion | flops 2109440 | bytes 9443328 | tf_op jit(solution)/shard_map/convert.3
  223.3 1.3 pad.124
  228.1 2.1 fusion.59
  232.2 3.1 convolution_convert_fusion.4
  235.3 3.5 %convolution_convert_fusion.3 = bf16[512,1024]{1,0:T(8,128)(2,1)} fusion(bf16[512,768]{1,0:T(8,128)(2,1)S(1)} %copy-done.39, bf16[1024,2304]{0,1:T(8,128)(2,1)} %all-gather.2.cloned.1.call-done), kind=kOutput, calls=%fused_computation.35 | convolution fusion | flops 805830656 | bytes 3407872 | tf_op jit(solution)/shard_map/dot_general | solution.py:34
  238.8 3.5 %convolution_convert_fusion = bf16[1024,1536]{1,0:T(8,128)(2,1)} fusion(bf16[512,1024]{1,0:T(8,128)(2,1)S(1)} %get-tuple-element.203, bf16[512,512]{1,0:T(8,128)(2,1)S(1)} %copy-done.7, bf16[512,1024]{1,0:T(8,128)(2,1)S(1)} %copy-done.11), kind=kOutput, calls=%fused_computation.1 | convolution fusion | flops 1615331328 | bytes 5767168 | tf_op jit(solution)/shard_map/dot_general | solution.py:30
  242.3 64.4 %reduce_all.1 = (f32[128,256]{1,0:T(8,128)}, f32[128,256]{1,0:T(8,128)}, f32[128,512]{1,0:T(8,128)}, f32[128,512]{1,0:T(8,128)}, f32[128,512]{1,0:T(8,128)}, /*i...) custom-call(bf16[8,128,1536]{2,1,0:T(8,128)(2,1)} %bitcast.216, ...), custom_call_target="tpu_custom_call" | custom-call | flops 30000001024 | bytes 16000000 | tf_op jit(solution)/shard_map/reduce_all/pallas_call | solution.py:569
  307.6 1.3 slice.162
  309.7 2.1 convert_reduce_fusion
  316.9 1.3 fusion.60
  (173 shorter events, 38.4 us)
Async XLA Ops:
  7.2 135.9 %all-gather.2.cloned.1.call-start = ((), (), s32[]{:S(2)}) async-start(), calls=%async_computation.1 | async-start | bytes 5308416 | tf_op jit(solution)/shard_map/all_gather | solution.py:829
  11.5 30.7 %copy-start.5 = (bf16[128,1024]{1,0:T(8,128)(2,1)S(1)}, bf16[128,1024]{1,0:T(8,128)(2,1)}, u32[]{:S(2)}) copy-start(bf16[128,1024]{1,0:T(8,128)(2,1)} %refs_1_.6) | copy-start | bytes 786436
  11.5 34.1 %copy-start.34 = (bf16[2]{0:T(256)(128)(2,1)S(1)}, bf16[2]{0:T(256)(128)(2,1)}, u32[]{:S(2)}) copy-start(bf16[2]{0:T(256)(128)(2,1)} %param.34) | copy-start | bytes 16
  11.5 34.1 %copy-start.35 = (bf16[2]{0:T(256)(128)(2,1)S(1)}, bf16[2]{0:T(256)(128)(2,1)}, u32[]{:S(2)}) copy-start(bf16[2]{0:T(256)(128)(2,1)} %param.33) | copy-start | bytes 16
  42.1 6.7 %copy-start = (bf16[4,128,1024]{2,1,0:T(8,128)(2,1)S(1)}, bf16[4,128,1024]{2,1,0:T(8,128)(2,1)}, u32[]{:S(2)}) copy-start(bf16[4,128,1024]{2,1,0:T(8,128)(2,1)} %get-tuple-element.54) | copy-start | bytes 3145732
  42.1 274.8 %reduce-scatter.2.cloned.1.call-start = ((), (), s32[]{:S(2)}) async-start(), calls=%async_computation.2 | async-start | bytes 5308416 | tf_op jit(solution)/shard_map/reduce_scatter | solution.py:890
  43.1 6.4 %copy-start.22 = (f32[8,1,128]{2,1,0:T(1,128)}, f32[8,1,128]{2,1,0:T(1,128)S(1)}, u32[]{:S(2)}) copy-start(f32[8,1,128]{2,1,0:T(1,128)S(1)} %slice.172) | copy-start | bytes 12292
  44.7 11.6 %copy-start.15 = (f32[8,16,128]{2,1,0:T(8,128)}, f32[8,16,128]{2,1,0:T(8,128)S(1)}, u32[]{:S(2)}) copy-start(f32[8,16,128]{2,1,0:T(8,128)S(1)} %convert_element_type.114) | copy-start | bytes 196612
  45.6 3.9 %copy-start.31 = (f32[2]{0:T(128)}, f32[2]{0:T(128)S(1)}, u32[]{:S(2)}) copy-start(f32[2]{0:T(128)S(1)} %convert_element_type.121) | copy-start | bytes 28
  45.6 3.9 %copy-start.32 = (f32[2]{0:T(128)}, f32[2]{0:T(128)S(1)}, u32[]{:S(2)}) copy-start(f32[2]{0:T(128)S(1)} %fusion.50) | copy-start | bytes 28
  49.0 4.9 %copy-start.4 = (bf16[4,128,1024]{2,1,0:T(8,128)(2,1)}, bf16[4,128,1024]{2,1,0:T(8,128)(2,1)S(1)}, u32[]{:S(2)}) copy-start(bf16[4,128,1024]{2,1,0:T(8,128)(2,1)S(1)} %multiply_convert_fusion.1) | copy-start | bytes 3145732
  51.2 2.8 copy-start.8
  143.1 4.1 %copy-start.36 = (bf16[4,128,1024]{2,1,0:T(8,128)(2,1)S(1)}, bf16[4,128,1024]{2,1,0:T(8,128)(2,1)}, u32[]{:S(2)}) copy-start(bf16[4,128,1024]{2,1,0:T(8,128)(2,1)} %get-tuple-element.66) | copy-start | bytes 3145732
  150.3 1.5 copy-start.41
  150.3 2.0 copy-start.37
  211.2 2.2 copy-start.3
  223.3 1.9 copy-start.10
  226.4 1.7 copy-start.12
  226.4 1.7 copy-start.23
  226.4 1.7 copy-start.28
  231.0 4.3 %copy-start.39 = (bf16[512,768]{1,0:T(8,128)(2,1)S(1)}, bf16[512,768]{1,0:T(8,128)(2,1)}, u32[]{:S(2)}) copy-start(bf16[512,768]{1,0:T(8,128)(2,1)} %copy-done.38) | copy-start | bytes 2359300
  235.3 3.5 %copy-start.11 = (bf16[512,1024]{1,0:T(8,128)(2,1)S(1)}, bf16[512,1024]{1,0:T(8,128)(2,1)}, u32[]{:S(2)}) copy-start(bf16[512,1024]{1,0:T(8,128)(2,1)} %pad.124) | copy-start | bytes 3145732
  306.8 5.1 %copy-start.6 = (bf16[128,1024]{1,0:T(8,128)(2,1)S(1)}, bf16[128,1024]{1,0:T(8,128)(2,1)}, u32[]{:S(2)}) copy-start(bf16[128,1024]{1,0:T(8,128)(2,1)} %refs_1_.6) | copy-start | bytes 786436
  306.8 5.1 %copy-start.30 = (f32[128]{0:T(128)S(1)}, f32[128]{0:T(128)}, u32[]{:S(2)}) copy-start(f32[128]{0:T(128)} %add_rsqrt_fusion.1) | copy-start | bytes 1540
  306.8 5.8 %copy-start.25 = (f32[16,128]{1,0:T(8,128)S(1)}, f32[16,128]{1,0:T(8,128)}, u32[]{:S(2)}) copy-start(f32[16,128]{1,0:T(8,128)} %get-tuple-element.85) | copy-start | bytes 24580
  306.8 8.2 %copy-start.14 = (f32[128,1024]{1,0:T(8,128)S(1)}, f32[128,1024]{1,0:T(8,128)}, u32[]{:S(2)}) copy-start(f32[128,1024]{1,0:T(8,128)} %get-tuple-element.63.refs_3_) | copy-start | bytes 1572868
  309.7 6.1 %copy-start.13 = (f32[128,1024]{1,0:T(8,128)S(1)}, f32[128,1024]{1,0:T(8,128)}, u32[]{:S(2)}) copy-start(f32[128,1024]{1,0:T(8,128)} %get-tuple-element.77) | copy-start | bytes 1572868
  316.9 4.0 %copy-start.21 = (f32[128,256]{1,0:T(8,128)S(1)}, f32[128,256]{1,0:T(8,128)}, u32[]{:S(2)}) copy-start(f32[128,256]{1,0:T(8,128)} %get-tuple-element.259) | copy-start | bytes 393220
  316.9 4.7 %copy-start.20 = (f32[128,256]{1,0:T(8,128)S(1)}, f32[128,256]{1,0:T(8,128)}, u32[]{:S(2)}) copy-start(f32[128,256]{1,0:T(8,128)} %get-tuple-element.260) | copy-start | bytes 393220
  316.9 5.3 %copy-start.19 = (f32[128,512]{1,0:T(8,128)S(1)}, f32[128,512]{1,0:T(8,128)}, u32[]{:S(2)}) copy-start(f32[128,512]{1,0:T(8,128)} %get-tuple-element.261) | copy-start | bytes 786436
  318.1 4.8 %copy-start.18 = (f32[128,512]{1,0:T(8,128)S(1)}, f32[128,512]{1,0:T(8,128)}, u32[]{:S(2)}) copy-start(f32[128,512]{1,0:T(8,128)} %get-tuple-element.262) | copy-start | bytes 786436
  318.1 5.5 %copy-start.17 = (f32[128,512]{1,0:T(8,128)S(1)}, f32[128,512]{1,0:T(8,128)}, u32[]{:S(2)}) copy-start(f32[128,512]{1,0:T(8,128)} %get-tuple-element.263) | copy-start | bytes 786436
  (12 other events, 14.9 us)
Sparse Core Ops, SparseCore 0:
  42.2 93.8 all-gather.1
  162.0 102.1 reduce-scatter.1
